TPU v7x, 1024 devices: a whole 8x8x8 slice. The times are simulated.
1024 devices in a mesh: row: 64 (over x, y), col: 16 (over z, core).
Axes of the slice: x: 8, y: 8, z: 8, core: 2. Of those that a mesh axis runs over, the one named last changes fastest.
Arguments:
- similarity: bfloat16 [7168, 7168], P('row', 'col'), may hold values from 0.0099487305 to 1
- in_pattern: int32 [56, 56], replicated, may hold values 0 or 1
- out_pattern: int32 [56, 56], replicated, may hold values 0 or 1
Outputs:
- inflated: bfloat16 [7168, 7168], P('row', 'col')
All inputs are finite; a program needn't handle non-finite values.
Results may differ from a plain program's by a relative error of at most 0.0029.
Values may be sent and summed in bfloat16 or wider, within the bound.
No kernel may reach another device: no remote copies, remote signals or barrier semaphores. Data moves between devices by JAX's collectives and lax.ppermute only.
A program may use at most 32 MiB of HBM per device.

v0:
```python
import jax
import jax.numpy as jnp
from jax import lax
from jax.sharding import PartitionSpec as P

BLK = 128


def local_mask(pattern, row_start, rows, col_start, cols):
    row_blocks = (row_start + jnp.arange(rows, dtype=jnp.int32)) // BLK
    col_blocks = (col_start + jnp.arange(cols, dtype=jnp.int32)) // BLK
    picked = jnp.take(jnp.take(pattern, row_blocks, axis=0), col_blocks, axis=1)
    forced = (row_blocks[:, None] == col_blocks[None, :]).astype(jnp.int32)
    return jnp.maximum(picked, forced) > 0


def shards(similarity, in_pattern, out_pattern):
    rows, cols = similarity.shape
    order = rows * lax.axis_size("row")
    row_start = lax.axis_index("row") * rows
    col_start = lax.axis_index("col") * cols
    masked = jnp.where(
        local_mask(in_pattern, row_start, rows, col_start, cols),
        similarity.astype(jnp.float32),
        jnp.float32(0.0),
    )
    in_sums = lax.psum(jnp.sum(masked, axis=0), "row")
    stochastic = (masked / in_sums[None, :]).astype(jnp.bfloat16)
    left_whole = lax.all_gather(stochastic, "col", axis=1, tiled=True)
    product = jnp.dot(
        left_whole,
        lax.all_gather(stochastic, "row", axis=0, tiled=True),
        preferred_element_type=jnp.float32,
    )
    expanded = jnp.where(
        local_mask(out_pattern, row_start, rows, col_start, cols), product, jnp.float32(0.0)
    )
    squared = expanded * expanded
    out_sums = lax.psum(jnp.sum(squared, axis=0), "row")
    return (jnp.float32(order) * squared / out_sums[None, :]).astype(jnp.bfloat16)


def solution(mesh):
    placed = (P("row", "col"), P(), P())
    return jax.shard_map(
        shards, mesh=mesh, in_specs=placed, out_specs=P("row", "col"), check_vma=False
    )
```

profile of v0, /device:TPU:8, one launch (start us, length us, event | category | flops | bytes accessed | tf_op | source)
XLA Modules:
  0.0 461.8 jit_solution(17983742227037189859)
XLA Ops:
  6.5 0.0 copy-start
  6.5 0.0 all-gather.3.cloned.1.call-start
  6.6 0.6 copy-done
  7.3 0.6 gather_fusion.2
  7.9 1.4 gather_fusion
  9.3 0.1 broadcast_select_fusion.1
  9.4 0.1 copy.10
  9.5 1.2 gather_fusion.3
  10.6 0.1 copy.11
  10.8 1.1 fusion.3
  11.8 142.2 %psum.14 = f32[448]{0:T(512)S(1)} all-reduce(f32[448]{0:T(512)S(1)} %get-tuple-element.6), channel_id=1, replica_groups=mesh['row'=64,'col'=16] {'row'}, use_global_device_ids=true, to_apply=%region_1.4 | all-reduce | flops 448 | bytes 3584 | tf_op jit(solution)/shard_map/psum | solution.py:27
  154.0 0.9 divide_convert_fusion.1
  155.0 0.0 copy-start.1
  155.0 0.8 copy.12
  155.8 0.0 all-gather.3.cloned.1.call-update
  155.8 0.0 all-gather.5.cloned.1.call-start
  155.8 0.0 copy-done.1
  155.8 0.7 all-gather.5.cloned.1.call-update
  156.5 0.1 copy.8
  156.6 1.2 gather_fusion.1
  157.8 0.1 copy.9
  157.9 50.2 %all-gather.3.cloned.1.call-done = bf16[112,7168]{0,1:T(8,128)(2,1)} async-done(((bf16[112,448]{0,1:T(8,128)(2,1)}), bf16[112,7168]{0,1:T(8,128)(2,1)}) %all-gather.3.cloned.1.call-update) | async-done | bytes 1605648 | tf_op jit(solution)/shard_map/all_gather | solution.py:29
  208.1 100.6 %all-gather.5.cloned.1.call-done = bf16[7168,448]{1,0:T(8,128)(2,1)} async-done(((bf16[112,448]{1,0:T(8,128)(2,1)}), bf16[7168,448]{1,0:T(8,128)(2,1)}) %all-gather.5.cloned.1.call-update) | async-done | bytes 6422544 | tf_op jit(solution)/shard_map/all_gather | solution.py:32
  308.7 5.0 %fusion.8 = (f32[448]{0:T(512)S(1)}, f32[112,448]{1,0:T(8,128)S(1)}) fusion(bf16[112,7168]{0,1:T(8,128)(2,1)} %all-gather.3.cloned.1.call-done, bf16[7168,448]{1,0:T(8,128)(2,1)} %all-gather.5.cloned.1.call-done, s32[448]{0:T(512)S(1)} %get-tuple-element.14, s32[112]{0:T(128)S(1)} %get-tuple-element.16, s32[448,112]{0,1:T(8,128)S(1)} %copy.9, ...), kind=kOutput, calls=%fused_computation.35 | convolution fusion | flops 719724096 | bytes 8434048 | tf_op jit(solution)/shard_map/dot_general | solution.py:30
  313.7 140.6 %psum.15 = f32[448]{0:T(512)S(1)} all-reduce(f32[448]{0:T(512)S(1)} %get-tuple-element.11), channel_id=1, replica_groups=mesh['row'=64,'col'=16] {'row'}, use_global_device_ids=true, to_apply=%region_3.6 | all-reduce | flops 448 | bytes 3584 | tf_op jit(solution)/shard_map/psum | solution.py:39
  454.3 0.7 divide_convert_fusion
  (6 shorter events, 0.1 us)
Async XLA Ops:
  6.5 0.7 copy-start
  6.5 201.6 %all-gather.3.cloned.1.call-start = ((), (), s32[]{:S(2)}) async-start(), calls=%async_computation | async-start | bytes 1949696 | tf_op jit(solution)/shard_map/all_gather | solution.py:29
  155.0 0.9 copy-start.1
  155.8 152.9 %all-gather.5.cloned.1.call-start = ((), (), s32[]{:S(2)}) async-start(), calls=%async_computation.1 | async-start | bytes 7454720 | tf_op jit(solution)/shard_map/all_gather | solution.py:32
Sparse Core Ops, SparseCore 0:
  155.9 52.1 all-gather.2
  212.3 96.3 all-gather.4
where the time goes:
time: 462 us
  blocking collectives  283 us (61%)
  waiting for transfers between devices  152 us (33%)
  between operations  13.5 us (3%)
  local copies, waits for them, and re-layouts  6.15 us (1%)
  matrix products  4.95 us (1%)
    psum x1, blocking collectives, shards(): in_sums = lax.psum(jnp.sum(masked, axis=0), 'row')  142 us
    psum x1, blocking collectives, shards(): out_sums = lax.psum(jnp.sum(squared, axis=0), 'row')  141 us
    all_gather x1, waiting for transfers between devices, shards(): lax.all_gather(stochastic, 'row', axis=0, tiled=True)  101 us
    all_gather x1, waiting for transfers between devices, shards(): left_whole = lax.all_gather(stochastic, 'col', axis=1, tiled=True)  50.2 us
  transfers between devices with their start and end apart: 2, of which 2 were waited for; matrix products, arithmetic and copies ran while one was open for 0% of the time, Pallas kernels for 0%

commit v1 on v0

v1 whole, which is shorter than its diff:
```python
import jax
import jax.numpy as jnp
from jax import lax
from jax.sharding import Mesh
from jax.sharding import PartitionSpec as P

BLK = 128
F32 = jnp.float32
BF16 = jnp.bfloat16
SCALE = 64.0


def local_mask(pattern, row_start, rows, col_start, cols):
    blocks = pattern.shape[0]
    row_blocks = (row_start + lax.broadcasted_iota(jnp.int32, (rows, blocks), 0)) // BLK
    pick_row = (row_blocks == lax.broadcasted_iota(jnp.int32, (rows, blocks), 1)).astype(BF16)
    col_blocks = (col_start + lax.broadcasted_iota(jnp.int32, (blocks, cols), 1)) // BLK
    pick_col = (col_blocks == lax.broadcasted_iota(jnp.int32, (blocks, cols), 0)).astype(BF16)
    eye = jnp.eye(blocks, dtype=jnp.int32)
    kept = jnp.maximum(pattern, eye).astype(BF16)
    by_row = jnp.dot(pick_row, kept, preferred_element_type=F32).astype(BF16)
    return jnp.dot(by_row, pick_col, preferred_element_type=F32) > 0.5


def split3(v):
    hi = v.astype(BF16)
    rest = v - hi.astype(F32)
    mid = rest.astype(BF16)
    low = (rest - mid.astype(F32)).astype(BF16)
    z = jnp.zeros_like(hi)
    return jnp.stack([hi, mid, low, z, z, z, z, z])


def body(similarity, in_pattern, out_pattern):
    rows, cols = similarity.shape
    x, y = lax.axis_index("x"), lax.axis_index("y")
    z, core = lax.axis_index("z"), lax.axis_index("core")
    n = lax.axis_size("x")
    order = rows * n * n
    row_start = (x * n + y) * rows
    col_start = (z * 2 + core) * cols
    in_mask = local_mask(in_pattern, row_start, rows, col_start, cols)
    masked = jnp.where(in_mask, similarity, jnp.zeros_like(similarity))
    swap = [(i * n + j, j * n + i) for i in range(n) for j in range(n)]
    left = lax.ppermute(masked, ("y", "z"), swap)
    right = lax.ppermute(masked, ("x", "y"), swap)
    own_sums = jnp.sum(masked.astype(F32), axis=0)
    part = jnp.sum(left.astype(F32), axis=0)
    right_all = lax.all_gather(jnp.concatenate([right, split3(part)]), "x")
    part = jnp.sum(right_all[:, rows : rows + 3].astype(F32), axis=(0, 1))
    left_all = lax.all_gather(jnp.concatenate([left, split3(part)]), "z")
    in_sums = jnp.sum(left_all[:, rows : rows + 3].astype(F32), axis=(0, 1))
    left_own = (left_all[:, :rows].astype(F32) / in_sums).astype(BF16).reshape(n * rows, cols)
    left_other = lax.ppermute(left_own, "core", [(0, 1), (1, 0)])
    halves = right_all[:, :rows].reshape(2, cols, cols)
    right_own = lax.dynamic_index_in_dim(halves, core, 0, False)
    right_other = lax.dynamic_index_in_dim(halves, 1 - core, 0, False)
    partial = jnp.dot(left_own, right_own, preferred_element_type=F32)
    partial = partial + jnp.dot(left_other, right_other, preferred_element_type=F32)
    partial = (partial * F32(SCALE)).astype(jnp.float16).reshape(n, rows, cols)
    partials = lax.all_to_all(partial, "y", 0, 0)
    product = jnp.sum(partials.astype(F32), axis=0) * F32(1.0 / SCALE)
    out_mask = local_mask(out_pattern, row_start, rows, col_start, cols)
    product = jnp.where(out_mask, product, F32(0.0))
    sums = jnp.concatenate([jnp.sum(product * product, axis=0), own_sums, jnp.zeros((1024 - 2 * cols,), F32)])
    sums = jnp.broadcast_to(sums.reshape(1, 8, 128), (n * n, 8, 128))
    sums = jnp.sum(lax.all_to_all(sums, ("x", "y"), 0, 0), axis=0).reshape(1024)
    own_in = sums[cols : 2 * cols]
    expanded = product / own_in
    out_sums = sums[:cols] / (own_in * own_in)
    return (F32(order) * (expanded * expanded) / out_sums).astype(BF16)


def solution(mesh):
    fine = Mesh(mesh.devices.reshape(8, 8, 8, 2), ("x", "y", "z", "core"))
    cells = P(("x", "y"), ("z", "core"))
    return jax.shard_map(
        body, mesh=fine, in_specs=(cells, P(), P()), out_specs=cells, check_vma=False
    )
```

time: 462 us -> 154 us (0.33)
  the two profiles are of different devices: /device:TPU:8 before, /device:TPU:16 now
where the time goes in v1:
time: 154 us; the launch traced here: 153 us
  blocking collectives  128 us (83%)
  starting transfers between devices  8.8 us (6%)
  waiting for transfers between devices  6.65 us (4%)
  local copies, waits for them, and re-layouts  3.73 us (2%)
  matrix products  3.29 us (2%)
  other arithmetic  2.34 us (2%)
    all_gather x1, blocking collectives, body(): right_all = lax.all_gather(jnp.concatenate([right, split3(part)]), 'x')  47.1 us
    all_to_all x1, blocking collectives, body(): partials = lax.all_to_all(partial, 'y', 0, 0)  31.1 us
    all_gather x1, blocking collectives, body(): left_all = lax.all_gather(jnp.concatenate([left, split3(part)]), 'z')  29.3 us
    all_to_all x1, blocking collectives, body(): sums = jnp.sum(lax.all_to_all(sums, ('x', 'y'), 0, 0), axis=0).reshape(1024)  20.9 us
    ppermute x1, starting transfers between devices, body(): left = lax.ppermute(masked, ('y', 'z'), swap)  4.96 us
    ppermute x1, waiting for transfers between devices, body(): right = lax.ppermute(masked, ('x', 'y'), swap)  4.4 us
  transfers between devices with their start and end apart: 3, of which 3 were waited for; matrix products, arithmetic and copies ran while one was open for 1% of the time, Pallas kernels for 0%

profile of v1, /device:TPU:16, one launch (start us, length us, event | category | flops | bytes accessed | tf_op | source)
XLA Modules:
  0.0 153.4 jit_solution(11728911138922773773)
XLA Ops:
  0.1 1.4 convert_reduce_fusion.3
  1.5 5.0 %collective-permute-start = (bf16[112,448]{1,0:T(8,128)(2,1)S(1)}, bf16[112,448]{1,0:T(8,128)(2,1)S(1)}, u32[]{:S(2)}, u32[]{:S(2)}) collective-permute-start(bf16[112,448]{1,0:T(8,128)(2,1)S(1)} %get-tuple-element.12), channel_id=1, source_target_pairs={{0,0},{2,16},{4,32},{6,48},{8,64},{10,80},{12,96},{14,112},{16,2},... | collective-permute-start | bytes 301064 | tf_op jit(solution)/shard_map/ppermute | solution.py:45
  6.5 1.9 %collective-permute-start.1 = (bf16[112,448]{1,0:T(8,128)(2,1)S(1)}, bf16[112,448]{1,0:T(8,128)(2,1)S(1)}, u32[]{:S(2)}, u32[]{:S(2)}) collective-permute-start(bf16[112,448]{1,0:T(8,128)(2,1)S(1)} %get-tuple-element.12), channel_id=1, source_target_pairs={{0,0},{16,128},{32,256},{48,384},{64,512},{80,640},{96,768},{112,8... | collective-permute-start | bytes 301064 | tf_op jit(solution)/shard_map/ppermute | solution.py:46
  8.4 1.2 collective-permute-done
  9.6 4.4 %collective-permute-done.1 = bf16[112,448]{1,0:T(8,128)(2,1)S(1)} collective-permute-done((bf16[112,448]{1,0:T(8,128)(2,1)S(1)}, bf16[112,448]{1,0:T(8,128)(2,1)S(1)}, u32[]{:S(2)}, u32[]{:S(2)}) %collective-permute-start.1) | collective-permute-done | bytes 100384 | tf_op jit(solution)/shard_map/ppermute | solution.py:46
  14.1 0.1 copy.16
  14.2 47.1 %all-gather.2 = bf16[8,120,448]{1,2,0:T(8,128)(2,1)S(1)} all-gather(bf16[1,120,448]{1,2,0:T(8,128)(2,1)S(1)} %copy.16), channel_id=2, replica_groups=mesh['x'=8,'y'=8,'z'=8,'core'=2] {'x'}, dimensions={0}, use_global_device_ids=true | all-gather | bytes 967680 | tf_op jit(solution)/shard_map/all_gather | solution.py:49
  61.3 0.4 convert_reduce_fusion.2
  61.8 0.1 copy.17
  61.9 29.3 %all-gather.3 = bf16[8,120,448]{1,2,0:T(8,128)(2,1)S(1)} all-gather(bf16[1,120,448]{1,2,0:T(8,128)(2,1)S(1)} %copy.17), channel_id=3, replica_groups=mesh['x'=8,'y'=8,'z'=8,'core'=2] {'z'}, dimensions={0}, use_global_device_ids=true | all-gather | bytes 967680 | tf_op jit(solution)/shard_map/all_gather | solution.py:51
  91.3 0.4 convert_reduce_fusion.1
  91.7 0.3 divide_convert_fusion
  92.0 0.6 copy.18
  92.6 0.7 reshape.83
  93.3 1.9 %collective-permute-start.2 = (bf16[896,448]{0,1:T(8,128)(2,1)S(1)}, bf16[896,448]{0,1:T(8,128)(2,1)S(1)}, u32[]{:S(2)}, u32[]{:S(2)}) collective-permute-start(bf16[896,448]{0,1:T(8,128)(2,1)S(1)} %reshape.83), channel_id=1, source_target_pairs={{0,1},{1,0},{2,3},{3,2},{4,5},{5,4},{6,7},{7,6},{8,9},{9,8},{10,11... | collective-permute-start | bytes 2408456 | tf_op jit(solution)/shard_map/ppermute | solution.py:54
  95.2 0.5 copy.24
  95.8 0.7 fusion.3
  96.5 1.1 collective-permute-done.2
  97.5 0.7 multiply_convert_fusion
  98.2 1.1 reshape.85
  99.3 0.3 copy.20
  99.6 0.0 copy-start
  99.6 31.1 %all_to_all.10 = f16[8,112,448]{1,2,0:T(8,128)(2,1)S(1)} all-to-all(f16[8,112,448]{1,2,0:T(8,128)(2,1)S(1)} %copy.20), channel_id=1, replica_groups=mesh['x'=8,'y'=8,'z'=8,'core'=2] {'y'}, dimensions={0} | all-to-all | bytes 1605632 | tf_op jit(solution)/shard_map/all_to_all | solution.py:61
  130.7 0.2 convert_reduce_fusion
  130.9 0.1 copy.22
  131.1 0.0 copy-done
  131.1 0.5 multiply_reduce_fusion
  131.6 0.1 maximum_bitcast_fusion
  131.7 20.9 %all_to_all.11 = f32[64,8,128]{2,1,0:T(8,128)S(1)} all-to-all(f32[64,8,128]{2,1,0:T(8,128)S(1)} %broadcast_in_dim.24), channel_id=1, replica_groups=mesh['x'=8,'y'=8,'z'=8,'core'=2] {'x','y'}, dimensions={0} | all-to-all | bytes 524288 | tf_op jit(solution)/shard_map/all_to_all | solution.py:67
  152.5 0.1 reduce_sum.75
  152.6 0.1 fusion.38
  152.7 0.7 divide_convert_fusion.1
  (15 shorter events, 0.2 us)
Async XLA Ops:
  1.5 8.1 %collective-permute-start = (bf16[112,448]{1,0:T(8,128)(2,1)S(1)}, bf16[112,448]{1,0:T(8,128)(2,1)S(1)}, u32[]{:S(2)}, u32[]{:S(2)}) collective-permute-start(bf16[112,448]{1,0:T(8,128)(2,1)S(1)} %get-tuple-element.12), channel_id=1, source_target_pairs={{0,0},{2,16},{4,32},{6,48},{8,64},{10,80},{12,96},{14,112},{16,2},... | collective-permute-start | bytes 301064 | tf_op jit(solution)/shard_map/ppermute | solution.py:45
  6.5 7.6 %collective-permute-start.1 = (bf16[112,448]{1,0:T(8,128)(2,1)S(1)}, bf16[112,448]{1,0:T(8,128)(2,1)S(1)}, u32[]{:S(2)}, u32[]{:S(2)}) collective-permute-start(bf16[112,448]{1,0:T(8,128)(2,1)S(1)} %get-tuple-element.12), channel_id=1, source_target_pairs={{0,0},{16,128},{32,256},{48,384},{64,512},{80,640},{96,768},{112,8... | collective-permute-start | bytes 301064 | tf_op jit(solution)/shard_map/ppermute | solution.py:46
  93.3 4.2 %collective-permute-start.2 = (bf16[896,448]{0,1:T(8,128)(2,1)S(1)}, bf16[896,448]{0,1:T(8,128)(2,1)S(1)}, u32[]{:S(2)}, u32[]{:S(2)}) collective-permute-start(bf16[896,448]{0,1:T(8,128)(2,1)S(1)} %reshape.83), channel_id=1, source_target_pairs={{0,1},{1,0},{2,3},{3,2},{4,5},{5,4},{6,7},{7,6},{8,9},{9,8},{10,11... | collective-permute-start | bytes 2408456 | tf_op jit(solution)/shard_map/ppermute | solution.py:54
  99.6 31.5 %copy-start = (s32[56,56]{1,0:T(8,128)S(1)}, s32[56,56]{1,0:T(8,128)}, u32[]{:S(2)}) copy-start(s32[56,56]{1,0:T(8,128)} %param.5) | copy-start | bytes 37636

commit v2 on v1

v2 whole, which is shorter than its diff:
```python
import jax
import jax.numpy as jnp
from jax import lax
from jax.sharding import Mesh
from jax.sharding import PartitionSpec as P

BLK = 128
F32 = jnp.float32
BF16 = jnp.bfloat16
SCALE = 64.0


def local_mask(pattern, row_start, rows, col_start, cols):
    blocks = pattern.shape[0]
    row_blocks = (row_start + lax.broadcasted_iota(jnp.int32, (rows, blocks), 0)) // BLK
    pick_row = (row_blocks == lax.broadcasted_iota(jnp.int32, (rows, blocks), 1)).astype(BF16)
    col_blocks = (col_start + lax.broadcasted_iota(jnp.int32, (blocks, cols), 1)) // BLK
    pick_col = (col_blocks == lax.broadcasted_iota(jnp.int32, (blocks, cols), 0)).astype(BF16)
    eye = jnp.eye(blocks, dtype=jnp.int32)
    kept = jnp.maximum(pattern, eye).astype(BF16)
    by_row = jnp.dot(pick_row, kept, preferred_element_type=F32).astype(BF16)
    return jnp.dot(by_row, pick_col, preferred_element_type=F32) > 0.5


def body(similarity, in_pattern, out_pattern):
    rows, cols = similarity.shape
    x, y = lax.axis_index("x"), lax.axis_index("y")
    z, core = lax.axis_index("z"), lax.axis_index("core")
    n = lax.axis_size("x")
    order = rows * n * n
    row_start = (x * n + y) * rows
    col_start = (z * 2 + core) * cols
    in_mask = local_mask(in_pattern, row_start, rows, col_start, cols)
    masked = jnp.where(in_mask, similarity, jnp.zeros_like(similarity))
    half = rows // 2
    low, high = masked[:half], masked[half:]
    front = y < n // 2
    first = lax.ppermute(
        jnp.where(front, low, high), "y", [(i, 2 * i) if i < n // 2 else (i, 2 * i - n + 1) for i in range(n)]
    )
    second = lax.ppermute(
        jnp.where(front, high, low), "y", [(i, 2 * i + 1) if i < n // 2 else (i, 2 * i - n) for i in range(n)]
    )
    own_sums = jnp.sum(masked.astype(F32), axis=0)
    left = jnp.broadcast_to(masked.T.reshape(n, 1, half, rows), (n, n, half, rows))
    left = lax.all_to_all(left.reshape(n * n, half, rows), ("y", "z"), 0, 0)
    left = left.reshape(n, cols, rows)
    part = jnp.sum(left.astype(F32), axis=(0, 2))
    part = jnp.concatenate([part, jnp.zeros((512 - cols,), F32)]).reshape(1, 4, 128)
    in_sums = lax.all_to_all(jnp.broadcast_to(part, (n, 4, 128)), "x", 0, 0)
    in_sums = jnp.sum(in_sums, axis=0).reshape(512)[:cols]
    right_all = lax.all_gather(jnp.concatenate([first, second]), "x")
    left_own = (left.astype(F32) / in_sums[None, :, None]).astype(BF16)
    left_other = lax.ppermute(left_own, "core", [(0, 1), (1, 0)])
    slot = (core + y) % 2
    halves = right_all.reshape(n, 2, half, cols)
    right_own = lax.dynamic_index_in_dim(halves, slot, 1, False).reshape(cols, cols)
    right_other = lax.dynamic_index_in_dim(halves, 1 - slot, 1, False).reshape(cols, cols)
    over_k = (((1,), (0,)), ((), ()))
    partial = lax.dot_general(left_own, right_own, over_k, preferred_element_type=F32)
    partial = partial + lax.dot_general(left_other, right_other, over_k, preferred_element_type=F32)
    partial = (partial * F32(SCALE)).astype(jnp.float16).reshape(n, rows, cols)
    partials = lax.all_to_all(partial, "y", 0, 0)
    product = jnp.sum(partials.astype(F32), axis=0) * F32(1.0 / SCALE)
    out_mask = local_mask(out_pattern, row_start, rows, col_start, cols)
    product = jnp.where(out_mask, product, F32(0.0))
    sums = jnp.concatenate([jnp.sum(product * product, axis=0), own_sums, jnp.zeros((1024 - 2 * cols,), F32)])
    sums = sums.reshape(8, 128)
    for axis in ("y", "x"):
        sums = jnp.sum(lax.all_to_all(jnp.broadcast_to(sums, (n, 8, 128)), axis, 0, 0), axis=0)
    sums = sums.reshape(1024)
    own_in = sums[cols : 2 * cols]
    expanded = product / own_in
    out_sums = sums[:cols] / (own_in * own_in)
    return (F32(order) * (expanded * expanded) / out_sums).astype(BF16)


def solution(mesh):
    fine = Mesh(mesh.devices.reshape(8, 8, 8, 2), ("x", "y", "z", "core"))
    cells = P(("x", "y"), ("z", "core"))
    return jax.shard_map(
        body, mesh=fine, in_specs=(cells, P(), P()), out_specs=cells, check_vma=False
    )
```

time: 154 us -> 154 us (level)
  the two profiles are of different devices: /device:TPU:16 before, /device:TPU:2 now
where the time goes in v2:
time: 154 us; the launch traced here: 153 us
  blocking collectives  76.4 us (50%)
  starting transfers between devices  39.5 us (26%)
  waiting for transfers between devices  28.1 us (18%)
  local copies, waits for them, and re-layouts  3.35 us (2%)
  matrix products  3.23 us (2%)
  other arithmetic  2.48 us (2%)
    all_to_all x1, blocking collectives, body(): partials = lax.all_to_all(partial, 'y', 0, 0)  28.9 us
    all_gather x1, blocking collectives, body(): right_all = lax.all_gather(jnp.concatenate([first, second]), 'x')  26.7 us
    all_to_all x1, starting transfers between devices, body(): left = lax.all_to_all(left.reshape(n * n, half, rows), ('y', 'z'), 0, 0)  23.4 us
    ppermute x1, waiting for transfers between devices, body(): lax.ppermute(jnp.where(front, high, low), 'y', [(i, 2 * i + 1) if i < n /...  21.9 us
    all_to_all x2, blocking collectives, body(): lax.all_to_all(jnp.broadcast_to(sums, (n, 8, 128)), axis, 0, 0)  20.7 us
    all_to_all x1, starting transfers between devices, body(): in_sums = lax.all_to_all(jnp.broadcast_to(part, (n, 4, 128)), 'x', 0, 0)  7.31 us
    ppermute x1, starting transfers between devices, body(): lax.ppermute(jnp.where(front, high, low), 'y', [(i, 2 * i + 1) if i < n /...  6.19 us
    all_to_all x1, waiting for transfers between devices, body(): in_sums = lax.all_to_all(jnp.broadcast_to(part, (n, 4, 128)), 'x', 0, 0)  5.01 us
  transfers between devices with their start and end apart: 5, of which 3 were waited for; matrix products, arithmetic and copies ran while one was open for 2% of the time, Pallas kernels for 0%

profile of v2, /device:TPU:2, one launch (start us, length us, event | category | flops | bytes accessed | tf_op | source)
XLA Modules:
  0.0 153.2 jit_solution(14780566494505978227)
XLA Ops:
  0.1 1.4 convert_reduce_fusion.2
  1.5 0.1 copy.11
  1.6 1.1 broadcast_in_dim.36
  2.7 23.4 %all-to-all-start = ((bf16[64,56,112]{2,1,0:T(8,128)(2,1)}), bf16[64,56,112]{2,1,0:T(8,128)(2,1)S(1)}, u32[]{:S(2)}, u32[]{:S(2)}) async-start(bf16[64,56,112]{2,1,0:T(8,128)(2,1)} %bitcast.2), calls=%async_computation | async-start | bytes 1835008 | tf_op jit(solution)/shard_map/all_to_all | solution.py:46
  26.1 0.7 collective-permute-start
  26.8 6.2 %collective-permute-start.1 = (bf16[56,448]{1,0:T(8,128)(2,1)S(1)}, bf16[56,448]{1,0:T(8,128)(2,1)S(1)}, u32[]{:S(2)}, u32[]{:S(2)}) collective-permute-start(bf16[56,448]{1,0:T(8,128)(2,1)S(1)} %get-tuple-element.8), channel_id=1, source_target_pairs={{0,16},{16,48},{32,80},{48,112},{64,0},{80,32},{96,64},{112,96},{1... | collective-permute-start | bytes 150536 | tf_op jit(solution)/shard_map/ppermute | solution.py:41
  33.0 0.0 collective-permute-done
  33.0 21.9 %collective-permute-done.1 = bf16[56,448]{1,0:T(8,128)(2,1)S(1)} collective-permute-done((bf16[56,448]{1,0:T(8,128)(2,1)S(1)}, bf16[56,448]{1,0:T(8,128)(2,1)S(1)}, u32[]{:S(2)}, u32[]{:S(2)}) %collective-permute-start.1) | collective-permute-done | bytes 50208 | tf_op jit(solution)/shard_map/ppermute | solution.py:41
  55.0 26.7 %all-gather = bf16[896,448]{1,0:T(8,128)(2,1)S(1)} all-gather(bf16[112,448]{1,0:T(8,128)(2,1)S(1)} %pad_maximum_fusion), channel_id=2, replica_groups=mesh['x'=8,'y'=8,'z'=8,'core'=2] {'x'}, dimensions={0}, use_global_device_ids=true | all-gather | bytes 903168 | tf_op jit(solution)/shard_map/all_gather | solution.py:52
  81.7 0.0 all-to-all-done
  81.7 0.5 convert_reduce_fusion.1
  82.2 0.1 reduce_sum.71
  82.3 0.6 broadcast_in_dim.38
  83.0 7.3 %all-to-all-start.1 = ((f32[8,4,128]{2,1,0:T(4,128)}), f32[8,4,128]{2,1,0:T(4,128)S(1)}, u32[]{:S(2)}, u32[]{:S(2)}) async-start(f32[8,4,128]{2,1,0:T(4,128)} %broadcast_in_dim.38), calls=%async_computation.1 | async-start | bytes 32768 | tf_op jit(solution)/shard_map/all_to_all | solution.py:50
  90.3 0.8 constant_dynamic-slice_fusion
  91.1 0.5 copy.14
  91.6 5.0 %all-to-all-done.1 = f32[8,4,128]{2,1,0:T(4,128)S(1)} async-done(((f32[8,4,128]{2,1,0:T(4,128)}), f32[8,4,128]{2,1,0:T(4,128)S(1)}, u32[]{:S(2)}, u32[]{:S(2)}) %all-to-all-start.1) | async-done | bytes 16416 | tf_op jit(solution)/shard_map/all_to_all | solution.py:50
  96.7 0.1 div.76
  96.7 0.2 divide_convert_fusion
  97.0 1.9 %collective-permute-start.2 = (bf16[8,448,112]{1,2,0:T(8,128)(2,1)S(1)}, bf16[8,448,112]{1,2,0:T(8,128)(2,1)S(1)}, u32[]{:S(2)}, u32[]{:S(2)}) collective-permute-start(bf16[8,448,112]{1,2,0:T(8,128)(2,1)S(1)} %divide_convert_fusion), channel_id=1, source_target_pairs={{0,1},{1,0},{2,3},{3,2},{4,5},{5,4},{6,7},{7,6},{8,9},{9,8},{10,11... | collective-permute-start | bytes 2408456 | tf_op jit(solution)/shard_map/ppermute | solution.py:54
  98.9 0.5 divide_convert_fusion.1
  99.5 0.0 copy-start
  99.5 0.7 fusion.33
  100.2 1.2 collective-permute-done.2
  101.4 0.0 copy-done
  101.4 0.6 multiply_convert_fusion
  102.0 0.0 copy-start.1
  102.0 28.9 %all_to_all.25 = f16[8,112,448]{2,1,0:T(8,128)(2,1)S(1)} all-to-all(f16[8,112,448]{2,1,0:T(8,128)(2,1)S(1)} %multiply_convert_fusion), channel_id=1, replica_groups=mesh['x'=8,'y'=8,'z'=8,'core'=2] {'y'}, dimensions={0} | all-to-all | bytes 1605632 | tf_op jit(solution)/shard_map/all_to_all | solution.py:63
  130.9 0.1 convert_reduce_fusion
  131.1 0.0 copy-done.1
  131.1 0.5 multiply_reduce_fusion
  131.6 0.1 maximum_bitcast_fusion
  131.7 10.4 %all_to_all.26 = f32[8,8,128]{2,1,0:T(8,128)S(1)} all-to-all(f32[8,8,128]{2,1,0:T(8,128)S(1)} %broadcast_in_dim.41), channel_id=1, replica_groups=mesh['x'=8,'y'=8,'z'=8,'core'=2] {'y'}, dimensions={0} | all-to-all | bytes 65536 | tf_op jit(solution)/shard_map/all_to_all | solution.py:70
  142.1 10.3 %all_to_all.27 = f32[8,8,128]{2,1,0:T(8,128)S(1)} all-to-all(f32[8,8,128]{2,1,0:T(8,128)S(1)} %broadcast_in_dim.42), channel_id=1, replica_groups=mesh['x'=8,'y'=8,'z'=8,'core'=2] {'x'}, dimensions={0} | all-to-all | bytes 65536 | tf_op jit(solution)/shard_map/all_to_all | solution.py:70
  152.4 0.1 fusion.28
  152.5 0.7 divide_convert_fusion.2
  (15 shorter events, 0.2 us)
Async XLA Ops:
  2.7 79.0 %all-to-all-start = ((bf16[64,56,112]{2,1,0:T(8,128)(2,1)}), bf16[64,56,112]{2,1,0:T(8,128)(2,1)S(1)}, u32[]{:S(2)}, u32[]{:S(2)}) async-start(bf16[64,56,112]{2,1,0:T(8,128)(2,1)} %bitcast.2), calls=%async_computation | async-start | bytes 1835008 | tf_op jit(solution)/shard_map/all_to_all | solution.py:46
  26.1 6.9 %collective-permute-start = (bf16[56,448]{1,0:T(8,128)(2,1)S(1)}, bf16[56,448]{1,0:T(8,128)(2,1)S(1)}, u32[]{:S(2)}, u32[]{:S(2)}) collective-permute-start(bf16[56,448]{1,0:T(8,128)(2,1)S(1)} %get-tuple-element.7), channel_id=1, source_target_pairs={{0,0},{16,32},{32,64},{48,96},{64,16},{80,48},{96,80},{112,112},{1... | collective-permute-start | bytes 150536 | tf_op jit(solution)/shard_map/ppermute | solution.py:38
  26.8 28.1 %collective-permute-start.1 = (bf16[56,448]{1,0:T(8,128)(2,1)S(1)}, bf16[56,448]{1,0:T(8,128)(2,1)S(1)}, u32[]{:S(2)}, u32[]{:S(2)}) collective-permute-start(bf16[56,448]{1,0:T(8,128)(2,1)S(1)} %get-tuple-element.8), channel_id=1, source_target_pairs={{0,16},{16,48},{32,80},{48,112},{64,0},{80,32},{96,64},{112,96},{1... | collective-permute-start | bytes 150536 | tf_op jit(solution)/shard_map/ppermute | solution.py:41
  83.0 13.7 %all-to-all-start.1 = ((f32[8,4,128]{2,1,0:T(4,128)}), f32[8,4,128]{2,1,0:T(4,128)S(1)}, u32[]{:S(2)}, u32[]{:S(2)}) async-start(f32[8,4,128]{2,1,0:T(4,128)} %broadcast_in_dim.38), calls=%async_computation.1 | async-start | bytes 32768 | tf_op jit(solution)/shard_map/all_to_all | solution.py:50
  97.0 4.4 %collective-permute-start.2 = (bf16[8,448,112]{1,2,0:T(8,128)(2,1)S(1)}, bf16[8,448,112]{1,2,0:T(8,128)(2,1)S(1)}, u32[]{:S(2)}, u32[]{:S(2)}) collective-permute-start(bf16[8,448,112]{1,2,0:T(8,128)(2,1)S(1)} %divide_convert_fusion), channel_id=1, source_target_pairs={{0,1},{1,0},{2,3},{3,2},{4,5},{5,4},{6,7},{7,6},{8,9},{9,8},{10,11... | collective-permute-start | bytes 2408456 | tf_op jit(solution)/shard_map/ppermute | solution.py:54
  99.5 1.9 %copy-start = (bf16[8,1,56,448]{3,2,1,0:T(8,128)(2,1)S(1)}, bf16[8,1,56,448]{3,2,1,0:T(8,128)(2,1)}, u32[]{:S(2)}) copy-start(bf16[8,1,56,448]{3,2,1,0:T(8,128)(2,1)} %get-tuple-element.5) | copy-start | bytes 1204228
  102.0 29.1 %copy-start.1 = (s32[56,56]{1,0:T(8,128)S(1)}, s32[56,56]{1,0:T(8,128)}, u32[]{:S(2)}) copy-start(s32[56,56]{1,0:T(8,128)} %param.5) | copy-start | bytes 37636

commit v3 on v1

v3 whole, which is shorter than its diff:
```python
import jax
import jax.numpy as jnp
from jax import lax
from jax.sharding import Mesh
from jax.sharding import PartitionSpec as P

BLK = 128
F32 = jnp.float32
BF16 = jnp.bfloat16
SCALE = 64.0


def local_mask(pattern, row_start, rows, col_start, cols):
    blocks = pattern.shape[0]
    row_blocks = (row_start + lax.broadcasted_iota(jnp.int32, (rows, blocks), 0)) // BLK
    pick_row = (row_blocks == lax.broadcasted_iota(jnp.int32, (rows, blocks), 1)).astype(BF16)
    col_blocks = (col_start + lax.broadcasted_iota(jnp.int32, (blocks, cols), 1)) // BLK
    pick_col = (col_blocks == lax.broadcasted_iota(jnp.int32, (blocks, cols), 0)).astype(BF16)
    eye = jnp.eye(blocks, dtype=jnp.int32)
    kept = jnp.maximum(pattern, eye).astype(BF16)
    by_row = jnp.dot(pick_row, kept, preferred_element_type=F32).astype(BF16)
    return jnp.dot(by_row, pick_col, preferred_element_type=F32) > 0.5


def send_all(v, axes, count):
    return jnp.sum(lax.all_to_all(jnp.broadcast_to(v, (count,) + v.shape), axes, 0, 0), axis=0)


def body(similarity, in_pattern, out_pattern):
    rows, cols = similarity.shape
    x, quad, spot = lax.axis_index("x"), lax.axis_index("quad"), lax.axis_index("spot")
    z, core = lax.axis_index("z"), lax.axis_index("core")
    n, m = lax.axis_size("x"), lax.axis_size("spot")
    order = rows * n * n
    row_start = (x * n + quad * m + spot) * rows
    col_start = (z * 2 + core) * cols
    in_mask = local_mask(in_pattern, row_start, rows, col_start, cols)
    masked = jnp.where(in_mask, similarity, jnp.zeros_like(similarity))
    own_sums = jnp.sum(masked.astype(F32), axis=0)

    left = lax.ppermute(masked, ("quad", "core"), [(0, 0), (1, 2), (2, 1), (3, 3)])
    left = jnp.broadcast_to(left.T.reshape(m, 1, rows, rows), (m, n, rows, rows))
    left = lax.all_to_all(left.reshape(m * n, rows, rows), ("spot", "z"), 0, 0)
    left = left.reshape(m, n, rows, rows)
    right = lax.all_gather(masked, "x", tiled=True)

    left, right = lax.optimization_barrier((left, right))
    other = lax.ppermute(left, "core", [(0, 1), (1, 0)])
    part = jnp.sum(left.astype(F32), axis=(0, 3))
    part = jnp.pad(part, ((0, 0), (0, 128 - rows)))
    in_sums = send_all(part, ("x", "core"), 2 * n)[:, :rows, None]

    def times(l):
        l = (l.astype(F32) / in_sums).astype(BF16).reshape(m, n * rows, rows)
        p = lax.dot_general(l, right, (((1,), (0,)), ((), ())), preferred_element_type=F32)
        return (p * F32(SCALE)).astype(jnp.float16)

    own, other = times(left), times(other)
    partial = jnp.where(core == 0, jnp.concatenate([own, other]), jnp.concatenate([other, own]))
    partials = lax.all_to_all(partial, ("quad", "spot"), 0, 0)
    product = jnp.sum(partials.astype(F32), axis=0) * F32(1.0 / SCALE)
    out_mask = local_mask(out_pattern, row_start, rows, col_start, cols)
    product = jnp.where(out_mask, product, F32(0.0))
    sums = jnp.concatenate([jnp.sum(product * product, axis=0), own_sums, jnp.zeros((1024 - 2 * cols,), F32)])
    sums = send_all(send_all(sums.reshape(8, 128), ("quad", "spot"), n), "x", n).reshape(1024)
    own_in = sums[cols : 2 * cols]
    expanded = product / own_in
    out_sums = sums[:cols] / (own_in * own_in)
    return (F32(order) * (expanded * expanded) / out_sums).astype(BF16)


def solution(mesh):
    fine = Mesh(mesh.devices.reshape(8, 2, 4, 8, 2), ("x", "quad", "spot", "z", "core"))
    cells = P(("x", "quad", "spot"), ("z", "core"))
    return jax.shard_map(
        body, mesh=fine, in_specs=(cells, P(), P()), out_specs=cells, check_vma=False
    )
```

time: 154 us -> 134 us (0.87)
  the two profiles are of different devices: /device:TPU:16 before, /device:TPU:2 now
where the time goes in v3:
time: 134 us; the launch traced here: 133 us
  blocking collectives  84.1 us (63%)
  starting transfers between devices  34.6 us (26%)
  waiting for transfers between devices  6.51 us (5%)
  matrix products  3.24 us (2%)
  local copies, waits for them, and re-layouts  2.46 us (2%)
  other arithmetic  2.17 us (2%)
    all_to_all x1, blocking collectives, body(): partials = lax.all_to_all(partial, ('quad', 'spot'), 0, 0)  36.7 us
    all_gather x1, blocking collectives, body(): right = lax.all_gather(masked, 'x', tiled=True)  26.5 us
    all_to_all x2, blocking collectives, send_all(): lax.all_to_all(jnp.broadcast_to(v, (count,) + v.shape), axes, 0, 0)  20.9 us
    all_to_all x1, starting transfers between devices, body(): left = lax.all_to_all(left.reshape(m * n, rows, rows), ('spot', 'z'), 0, 0)  20.5 us
    all_to_all x1, starting transfers between devices, send_all(): lax.all_to_all(jnp.broadcast_to(v, (count,) + v.shape), axes, 0, 0)  7.13 us
    all_to_all x1, waiting for transfers between devices, send_all(): lax.all_to_all(jnp.broadcast_to(v, (count,) + v.shape), axes, 0, 0)  6.5 us
    ppermute x1, starting transfers between devices, body(): other = lax.ppermute(left, 'core', [(0, 1), (1, 0)])  6.34 us
  transfers between devices with their start and end apart: 4, of which 1 were waited for; matrix products, arithmetic and copies ran while one was open for 1% of the time, Pallas kernels for 0%

profile of v3, /device:TPU:2, one launch (start us, length us, event | category | flops | bytes accessed | tf_op | source)
XLA Modules:
  0.0 133.2 jit_solution(11262836557851395611)
XLA Ops:
  0.1 1.4 %convert_reduce_fusion.2 = (f32[448]{0:T(512)S(1)}, bf16[112,448]{1,0:T(8,128)(2,1)S(1)}) fusion(bf16[112,448]{1,0:T(8,128)(2,1)} %param.3, s32[448]{0:T(512)S(1)} %get-tuple-element.17, s32[448]{0:T(512)S(1)} %get-tuple-element.18, pred[448]{0:T(512)(128)(4,1)S(1)} %fusion.33, s32[112]{0:T(128)S(1)} %get-tuple-element.19, s32[112]{0:T(128)S(1)} %get-tuple-element.20, ...), kind=kOutput, calls=%fused_computation.19 | convolution fusion | flops 6603968 | bytes 220080 | tf_op jit(solution)/shard_map/dot_general | solution.py:22
  1.5 0.7 collective-permute-start
  2.2 0.0 collective-permute-done
  2.2 0.1 copy.21
  2.3 1.1 broadcast_in_dim.30
  3.4 20.5 %all-to-all-start = ((bf16[32,112,112]{2,1,0:T(8,128)(2,1)}), bf16[32,112,112]{2,1,0:T(8,128)(2,1)S(1)}, u32[]{:S(2)}, u32[]{:S(2)}) async-start(bf16[32,112,112]{2,1,0:T(8,128)(2,1)} %bitcast.2), calls=%async_computation | async-start | bytes 1835008 | tf_op jit(solution)/shard_map/all_to_all | solution.py:43
  23.8 26.5 %all_gather.3 = bf16[896,448]{1,0:T(8,128)(2,1)S(1)} all-gather(bf16[112,448]{1,0:T(8,128)(2,1)S(1)} %get-tuple-element.14), channel_id=1, replica_groups=mesh['x'=8,'quad'=2,'spot'=4,'z'=8,'core'=2] {'x'}, dimensions={0}, use_global_device_ids=true | all-gather | bytes 903168 | tf_op jit(solution)/shard_map/all_gather | solution.py:45
  50.3 0.0 all-to-all-done
  50.3 6.3 %collective-permute-start.1 = (bf16[4,8,112,112]{3,2,1,0:T(8,128)(2,1)S(1)}, bf16[4,8,112,112]{3,2,1,0:T(8,128)(2,1)S(1)}, u32[]{:S(2)}, u32[]{:S(2)}) collective-permute-start(bf16[4,8,112,112]{3,2,1,0:T(8,128)(2,1)S(1)} %bitcast.18), channel_id=1, source_target_pairs={{0,1},{1,0},{2,3},{3,2},{4,5},{5,4},{6,7},{7,6},{8,9},{9,8},{10,11... | collective-permute-start | bytes 2408456 | tf_op jit(solution)/shard_map/ppermute | solution.py:48
  56.7 0.3 convert_reduce_fusion
  57.0 0.6 broadcast_in_dim.31
  57.6 7.1 %all-to-all-start.1 = ((f32[16,8,128]{2,1,0:T(8,128)}), f32[16,8,128]{2,1,0:T(8,128)S(1)}, u32[]{:S(2)}, u32[]{:S(2)}) async-start(f32[16,8,128]{2,1,0:T(8,128)} %broadcast_in_dim.31), calls=%async_computation.1 | async-start | bytes 131072 | tf_op jit(solution)/shard_map/all_to_all | solution.py:26
  64.7 6.5 %all-to-all-done.1 = f32[16,8,128]{2,1,0:T(8,128)S(1)} async-done(((f32[16,8,128]{2,1,0:T(8,128)}), f32[16,8,128]{2,1,0:T(8,128)S(1)}, u32[]{:S(2)}, u32[]{:S(2)}) %all-to-all-start.1) | async-done | bytes 65568 | tf_op jit(solution)/shard_map/all_to_all | solution.py:26
  71.3 0.0 collective-permute-done.1
  71.3 0.5 fusion
  71.7 0.7 fusion.1
  72.4 0.7 fusion.2
  73.1 0.4 maximum_select_fusion
  73.5 36.7 %all_to_all.25 = f16[8,112,448]{2,1,0:T(8,128)(2,1)S(1)} all-to-all(f16[8,112,448]{2,1,0:T(8,128)(2,1)S(1)} %maximum_select_fusion), channel_id=1, replica_groups=mesh['x'=8,'quad'=2,'spot'=4,'z'=8,'core'=2] {'quad','spot'}, dimensions={0} | all-to-all | bytes 1605632 | tf_op jit(solution)/shard_map/all_to_all | solution.py:60
  110.2 0.0 copy-start
  110.2 0.1 convert_reduce_fusion.1
  110.3 0.6 copy-done
  110.9 0.5 multiply_reduce_fusion
  111.4 0.1 maximum_bitcast_fusion
  111.5 10.4 %all_to_all.26 = f32[8,8,128]{2,1,0:T(8,128)S(1)} all-to-all(f32[8,8,128]{2,1,0:T(8,128)S(1)} %broadcast_in_dim.34), channel_id=1, replica_groups=mesh['x'=8,'quad'=2,'spot'=4,'z'=8,'core'=2] {'quad','spot'}, dimensions={0} | all-to-all | bytes 65536 | tf_op jit(solution)/shard_map/all_to_all | solution.py:26
  121.9 10.5 %all_to_all.27 = f32[8,8,128]{2,1,0:T(8,128)S(1)} all-to-all(f32[8,8,128]{2,1,0:T(8,128)S(1)} %broadcast_in_dim.35), channel_id=1, replica_groups=mesh['x'=8,'quad'=2,'spot'=4,'z'=8,'core'=2] {'x'}, dimensions={0} | all-to-all | bytes 65536 | tf_op jit(solution)/shard_map/all_to_all | solution.py:26
  132.4 0.1 fusion.34
  132.5 0.7 divide_convert_fusion.1
  (11 shorter events, 0.1 us)
Async XLA Ops:
  1.5 0.7 collective-permute-start
  3.4 47.0 %all-to-all-start = ((bf16[32,112,112]{2,1,0:T(8,128)(2,1)}), bf16[32,112,112]{2,1,0:T(8,128)(2,1)S(1)}, u32[]{:S(2)}, u32[]{:S(2)}) async-start(bf16[32,112,112]{2,1,0:T(8,128)(2,1)} %bitcast.2), calls=%async_computation | async-start | bytes 1835008 | tf_op jit(solution)/shard_map/all_to_all | solution.py:43
  50.3 20.9 %collective-permute-start.1 = (bf16[4,8,112,112]{3,2,1,0:T(8,128)(2,1)S(1)}, bf16[4,8,112,112]{3,2,1,0:T(8,128)(2,1)S(1)}, u32[]{:S(2)}, u32[]{:S(2)}) collective-permute-start(bf16[4,8,112,112]{3,2,1,0:T(8,128)(2,1)S(1)} %bitcast.18), channel_id=1, source_target_pairs={{0,1},{1,0},{2,3},{3,2},{4,5},{5,4},{6,7},{7,6},{8,9},{9,8},{10,11... | collective-permute-start | bytes 2408456 | tf_op jit(solution)/shard_map/ppermute | solution.py:48
  57.6 13.6 %all-to-all-start.1 = ((f32[16,8,128]{2,1,0:T(8,128)}), f32[16,8,128]{2,1,0:T(8,128)S(1)}, u32[]{:S(2)}, u32[]{:S(2)}) async-start(f32[16,8,128]{2,1,0:T(8,128)} %broadcast_in_dim.31), calls=%async_computation.1 | async-start | bytes 131072 | tf_op jit(solution)/shard_map/all_to_all | solution.py:26
  110.2 0.7 copy-start

commit v4 on v3

--- a/solution.py
+++ b/solution.py
@@ -26,12 +26,11 @@
     return jnp.sum(lax.all_to_all(jnp.broadcast_to(v, (count,) + v.shape), axes, 0, 0), axis=0)
 
 
-def body(similarity, in_pattern, out_pattern):
+def multiply(similarity, in_pattern):
     rows, cols = similarity.shape
     x, quad, spot = lax.axis_index("x"), lax.axis_index("quad"), lax.axis_index("spot")
     z, core = lax.axis_index("z"), lax.axis_index("core")
     n, m = lax.axis_size("x"), lax.axis_size("spot")
-    order = rows * n * n
     row_start = (x * n + quad * m + spot) * rows
     col_start = (z * 2 + core) * cols
     in_mask = local_mask(in_pattern, row_start, rows, col_start, cols)
@@ -46,23 +45,30 @@
 
     left, right = lax.optimization_barrier((left, right))
     other = lax.ppermute(left, "core", [(0, 1), (1, 0)])
-    part = jnp.sum(left.astype(F32), axis=(0, 3))
+    part = jnp.sum(left.astype(F32), axis=(0, 3)) + jnp.sum(other.astype(F32), axis=(0, 3))
     part = jnp.pad(part, ((0, 0), (0, 128 - rows)))
-    in_sums = send_all(part, ("x", "core"), 2 * n)[:, :rows, None]
+    in_sums = send_all(part, "x", n)[:, :rows, None]
+    left = jnp.where(core == 0, jnp.concatenate([left, other]), jnp.concatenate([other, left]))
+    left = (left.astype(F32) / in_sums).astype(BF16).reshape(n, n * rows, rows)
+    partial = lax.dot_general(left, right, (((1,), (0,)), ((), ())), preferred_element_type=F32)
+    partial = (partial * F32(SCALE)).astype(jnp.float16)
+    return partial.reshape(n * rows, cols), own_sums.reshape(1, cols)
 
-    def times(l):
-        l = (l.astype(F32) / in_sums).astype(BF16).reshape(m, n * rows, rows)
-        p = lax.dot_general(l, right, (((1,), (0,)), ((), ())), preferred_element_type=F32)
-        return (p * F32(SCALE)).astype(jnp.float16)
 
-    own, other = times(left), times(other)
-    partial = jnp.where(core == 0, jnp.concatenate([own, other]), jnp.concatenate([other, own]))
-    partials = lax.all_to_all(partial, ("quad", "spot"), 0, 0)
+def finish(partial, own_sums, out_pattern):
+    x, y = lax.axis_index("x"), lax.axis_index("y")
+    z, core = lax.axis_index("z"), lax.axis_index("core")
+    n = lax.axis_size("x")
+    rows, cols = partial.shape[0] // n, partial.shape[1]
+    order = rows * n * n
+    partials = lax.all_to_all(partial.reshape(n, rows, cols), "y", 0, 0)
     product = jnp.sum(partials.astype(F32), axis=0) * F32(1.0 / SCALE)
-    out_mask = local_mask(out_pattern, row_start, rows, col_start, cols)
+    out_mask = local_mask(out_pattern, (x * n + y) * rows, rows, (z * 2 + core) * cols, cols)
     product = jnp.where(out_mask, product, F32(0.0))
-    sums = jnp.concatenate([jnp.sum(product * product, axis=0), own_sums, jnp.zeros((1024 - 2 * cols,), F32)])
-    sums = send_all(send_all(sums.reshape(8, 128), ("quad", "spot"), n), "x", n).reshape(1024)
+    sums = jnp.concatenate(
+        [jnp.sum(product * product, axis=0), own_sums.reshape(cols), jnp.zeros((1024 - 2 * cols,), F32)]
+    )
+    sums = send_all(send_all(sums.reshape(8, 128), "y", n), "x", n).reshape(1024)
     own_in = sums[cols : 2 * cols]
     expanded = product / own_in
     out_sums = sums[:cols] / (own_in * own_in)
@@ -70,8 +76,18 @@
 
 
 def solution(mesh):
-    fine = Mesh(mesh.devices.reshape(8, 2, 4, 8, 2), ("x", "quad", "spot", "z", "core"))
-    cells = P(("x", "quad", "spot"), ("z", "core"))
-    return jax.shard_map(
-        body, mesh=fine, in_specs=(cells, P(), P()), out_specs=cells, check_vma=False
+    cut = Mesh(mesh.devices.reshape(8, 2, 4, 8, 2), ("x", "quad", "spot", "z", "core"))
+    whole = Mesh(mesh.devices.reshape(8, 8, 8, 2), ("x", "y", "z", "core"))
+    cells_cut = P(("x", "quad", "spot"), ("z", "core"))
+    cells = P(("x", "y"), ("z", "core"))
+    first = jax.shard_map(
+        multiply, mesh=cut, in_specs=(cells_cut, P()), out_specs=(cells_cut, cells_cut), check_vma=False
     )
+    second = jax.shard_map(
+        finish, mesh=whole, in_specs=(cells, cells, P()), out_specs=cells, check_vma=False
+    )
+
+    def step(similarity, in_pattern, out_pattern):
+        return second(*first(similarity, in_pattern), out_pattern)
+
+    return step

time: 134 us -> 136 us (1.015)
  blocking collectives: 84.1 us -> 47.4 us
  waiting for transfers between devices: 6.51 us -> 32.1 us
  starting transfers between devices: 34.6 us -> 45.3 us
    all_to_all x1 -> x0, blocking collectives: 36.7 us -> none  [body(): partials = lax.all_to_all(partial, ('quad', 'spot'), 0, 0)]
    all_to_all x1 -> x2, waiting for transfers between devices: 0.01 us -> 24.7 us  [the longest x1 24.7 us: finish(): partials = lax.all_to_all(partial.reshape(n, rows, cols), 'y', 0, 0)]
    all_to_all x1 -> x2, starting transfers between devices: 20.5 us -> 31.3 us  [the longest x1 20.5 us: multiply(): left = lax.all_to_all(left.reshape(m * n, rows, rows), ('spot', 'z'), 0, 0)]
    ppermute x2, waiting for transfers between devices: 0.01 us -> 1.82 us  [the longest x1 1.82 us: multiply(): other = lax.ppermute(left, 'core', [(0, 1), (1, 0)])]
  transfers between devices with their start and end apart: 4 -> 5, of which waited for: 1 -> 3; matrix products, arithmetic and copies ran while one was open for 1% -> 1% of each run, Pallas kernels for 0% -> 0%
where the time goes in v4:
time: 136 us; the launch traced here: 135 us
  blocking collectives  47.4 us (35%)
  starting transfers between devices  45.3 us (33%)
  waiting for transfers between devices  32.1 us (24%)
  matrix products  4.56 us (3%)
  local copies, waits for them, and re-layouts  3.09 us (2%)
  other arithmetic  2.37 us (2%)
    all_gather x1, blocking collectives, multiply(): right = lax.all_gather(masked, 'x', tiled=True)  26.5 us
    all_to_all x1, waiting for transfers between devices, finish(): partials = lax.all_to_all(partial.reshape(n, rows, cols), 'y', 0, 0)  24.7 us
    all_to_all x2, blocking collectives, send_all(): lax.all_to_all(jnp.broadcast_to(v, (count,) + v.shape), axes, 0, 0)  20.9 us
    all_to_all x1, starting transfers between devices, multiply(): left = lax.all_to_all(left.reshape(m * n, rows, rows), ('spot', 'z'), 0, 0)  20.5 us
    all_to_all x1, starting transfers between devices, finish(): partials = lax.all_to_all(partial.reshape(n, rows, cols), 'y', 0, 0)  10.8 us
    all_to_all x1, starting transfers between devices, send_all(): lax.all_to_all(jnp.broadcast_to(v, (count,) + v.shape), axes, 0, 0)  7.12 us
    ppermute x1, starting transfers between devices, multiply(): other = lax.ppermute(left, 'core', [(0, 1), (1, 0)])  6.27 us
    all_to_all x1, waiting for transfers between devices, send_all(): lax.all_to_all(jnp.broadcast_to(v, (count,) + v.shape), axes, 0, 0)  5.5 us
  transfers between devices with their start and end apart: 5, of which 3 were waited for; matrix products, arithmetic and copies ran while one was open for 1% of the time, Pallas kernels for 0%

profile of v4, /device:TPU:2, one launch (start us, length us, event | category | flops | bytes accessed | tf_op | source)
XLA Modules:
  0.0 135.1 jit_solution(4666090597073211149)
XLA Ops:
  0.0 0.0 copy-start.1
  0.1 0.0 copy-start.3
  0.1 0.0 copy-start.6
  0.1 2.0 %convert_reduce_fusion.3 = (f32[448]{0:T(512)}, bf16[112,448]{1,0:T(8,128)(2,1)S(1)}) fusion(bf16[112,448]{1,0:T(8,128)(2,1)} %param.5, s32[448]{0:T(512)S(1)} %get-tuple-element.17, s32[448]{0:T(512)S(1)} %get-tuple-element.18, pred[448]{0:T(512)(128)(4,1)S(1)} %fusion.31, s32[112]{0:T(128)S(1)} %get-tuple-element.19, s32[112]{0:T(128)S(1)} %get-tuple-element.20, ...), kind=kOutput, calls=%fused_computation.17 | convolution fusion | flops 6603968 | bytes 220080 | tf_op jit(solution)/shard_map/dot_general | solution.py:22
  2.1 0.7 collective-permute-start
  2.8 0.0 collective-permute-done
  2.8 0.0 copy-done.1
  2.8 0.0 copy-done.3
  2.8 0.0 copy-done.6
  2.8 0.1 copy.23
  2.9 1.1 broadcast_in_dim.30
  4.0 20.5 %all-to-all-start = ((bf16[32,112,112]{2,1,0:T(8,128)(2,1)}), bf16[32,112,112]{2,1,0:T(8,128)(2,1)S(1)}, u32[]{:S(2)}, u32[]{:S(2)}) async-start(bf16[32,112,112]{2,1,0:T(8,128)(2,1)} %bitcast.2), calls=%async_computation | async-start | bytes 1835008 | tf_op jit(solution)/shard_map/all_to_all | solution.py:42
  24.5 26.5 %all_gather.3 = bf16[896,448]{1,0:T(8,128)(2,1)S(1)} all-gather(bf16[112,448]{1,0:T(8,128)(2,1)S(1)} %get-tuple-element.14), channel_id=1, replica_groups=mesh['x'=8,'quad'=2,'spot'=4,'z'=8,'core'=2] {'x'}, dimensions={0}, use_global_device_ids=true | all-gather | bytes 903168 | tf_op jit(solution)/shard_map/all_gather | solution.py:44
  51.0 0.0 all-to-all-done
  51.0 6.3 %collective-permute-start.1 = (bf16[4,8,112,112]{3,2,1,0:T(8,128)(2,1)S(1)}, bf16[4,8,112,112]{3,2,1,0:T(8,128)(2,1)S(1)}, u32[]{:S(2)}, u32[]{:S(2)}) collective-permute-start(bf16[4,8,112,112]{3,2,1,0:T(8,128)(2,1)S(1)} %bitcast.13), channel_id=1, source_target_pairs={{0,1},{1,0},{2,3},{3,2},{4,5},{5,4},{6,7},{7,6},{8,9},{9,8},{10,11... | collective-permute-start | bytes 2408456 | tf_op jit(solution)/shard_map/ppermute | solution.py:47
  57.3 0.3 convert_reduce_fusion.2
  57.5 1.8 %collective-permute-done.1 = bf16[4,8,112,112]{3,2,1,0:T(8,128)(2,1)S(1)} collective-permute-done((bf16[4,8,112,112]{3,2,1,0:T(8,128)(2,1)S(1)}, bf16[4,8,112,112]{3,2,1,0:T(8,128)(2,1)S(1)}, u32[]{:S(2)}, u32[]{:S(2)}) %collective-permute-start.1) | collective-permute-done | bytes 802848 | tf_op jit(solution)/shard_map/ppermute | solution.py:47
  59.3 0.3 convert_reduce_fusion.1
  59.6 0.6 broadcast_in_dim.31
  60.2 7.1 %all-to-all-start.1 = ((f32[8,8,128]{2,1,0:T(8,128)}), f32[8,8,128]{2,1,0:T(8,128)}, u32[]{:S(2)}, u32[]{:S(2)}) async-start(f32[8,8,128]{2,1,0:T(8,128)} %broadcast_in_dim.31), calls=%async_computation.1 | async-start | bytes 65536 | tf_op jit(solution)/shard_map/all_to_all | solution.py:26
  67.4 0.6 copy.17
  67.9 0.6 copy.18
  68.5 5.5 %all-to-all-done.1 = f32[8,8,128]{2,1,0:T(8,128)} async-done(((f32[8,8,128]{2,1,0:T(8,128)}), f32[8,8,128]{2,1,0:T(8,128)}, u32[]{:S(2)}, u32[]{:S(2)}) %all-to-all-start.1) | async-done | bytes 32800 | tf_op jit(solution)/shard_map/all_to_all | solution.py:26
  74.0 0.8 reduce_sum.74
  74.8 0.1 div.90
  74.9 2.1 %multiply_convert_fusion = f16[8,112,448]{2,1,0:T(8,128)(2,1)} fusion(bf16[4,896,112]{1,2,0:T(8,128)(2,1)S(1)} %copy.18, bf16[4,896,112]{1,2,0:T(8,128)(2,1)S(1)} %copy.17, f32[896]{0:T(1024)S(1)} %div.90, pred[]{:T(512)S(6)} %eq.21, bf16[896,448]{1,0:T(8,128)(2,1)S(1)} %all_gather.3), kind=kOutput, calls=%fused_computation.2 | convolution fusion | flops 724942848 | bytes 3214849 | tf_op jit(solution)/shard_map/dot_general | solution.py:53
  76.9 10.8 %all-to-all-start.2 = ((f16[8,112,448]{2,1,0:T(8,128)(2,1)}), f16[8,112,448]{2,1,0:T(8,128)(2,1)S(1)}, u32[]{:S(2)}, u32[]{:S(2)}) async-start(f16[8,112,448]{2,1,0:T(8,128)(2,1)} %multiply_convert_fusion), calls=%async_computation.2 | async-start | bytes 1835008 | tf_op jit(solution)/shard_map/all_to_all | solution.py:64
  87.8 0.0 copy-start
  87.8 0.0 copy-start.2
  87.8 0.0 copy-start.4
  87.8 0.0 copy-start.7
  87.8 0.0 copy-start.5
  87.9 24.7 %all-to-all-done.2 = f16[8,112,448]{2,1,0:T(8,128)(2,1)S(1)} async-done(((f16[8,112,448]{2,1,0:T(8,128)(2,1)}), f16[8,112,448]{2,1,0:T(8,128)(2,1)S(1)}, u32[]{:S(2)}, u32[]{:S(2)}) %all-to-all-start.2) | async-done | bytes 802848 | tf_op jit(solution)/shard_map/all_to_all | solution.py:64
  112.6 0.1 convert_reduce_fusion
  112.8 0.0 copy-done
  112.8 0.0 copy-done.2
  112.8 0.0 copy-done.4
  112.8 0.0 copy-done.7
  112.8 0.5 multiply_reduce_fusion
  113.3 0.0 copy-done.5
  113.3 0.1 maximum_bitcast_fusion
  113.4 10.4 %all_to_all.25 = f32[8,8,128]{2,1,0:T(8,128)S(1)} all-to-all(f32[8,8,128]{2,1,0:T(8,128)S(1)} %broadcast_in_dim.34), channel_id=1, replica_groups=mesh['x'=8,'quad'=2,'spot'=4,'z'=8,'core'=2] {'quad','spot'}, dimensions={0} | all-to-all | bytes 65536 | tf_op jit(solution)/shard_map/all_to_all | solution.py:26
  123.8 10.5 %all_to_all.26 = f32[8,8,128]{2,1,0:T(8,128)S(1)} all-to-all(f32[8,8,128]{2,1,0:T(8,128)S(1)} %broadcast_in_dim.35), channel_id=1, replica_groups=mesh['x'=8,'quad'=2,'spot'=4,'z'=8,'core'=2] {'x'}, dimensions={0} | all-to-all | bytes 65536 | tf_op jit(solution)/shard_map/all_to_all | solution.py:26
  134.3 0.1 fusion.33
  134.4 0.7 divide_convert_fusion.4
  (13 shorter events, 0.1 us)
Async XLA Ops:
  0.0 2.7 %copy-start.1 = (s32[448]{0:T(512)}, s32[448]{0:T(512)S(1)}, u32[]{:S(2)}) copy-start(s32[448]{0:T(512)S(1)} %get-tuple-element.17) | copy-start | bytes 5380
  0.1 2.7 %copy-start.3 = (s32[448]{0:T(512)}, s32[448]{0:T(512)S(1)}, u32[]{:S(2)}) copy-start(s32[448]{0:T(512)S(1)} %get-tuple-element.18) | copy-start | bytes 5380
  0.1 2.7 %copy-start.6 = (pred[448]{0:T(512)(128)(4,1)}, pred[448]{0:T(512)(128)(4,1)S(1)}, u32[]{:S(2)}) copy-start(pred[448]{0:T(512)(128)(4,1)S(1)} %fusion.31) | copy-start | bytes 1348
  2.1 0.7 collective-permute-start
  4.0 47.0 %all-to-all-start = ((bf16[32,112,112]{2,1,0:T(8,128)(2,1)}), bf16[32,112,112]{2,1,0:T(8,128)(2,1)S(1)}, u32[]{:S(2)}, u32[]{:S(2)}) async-start(bf16[32,112,112]{2,1,0:T(8,128)(2,1)} %bitcast.2), calls=%async_computation | async-start | bytes 1835008 | tf_op jit(solution)/shard_map/all_to_all | solution.py:42
  51.0 8.4 %collective-permute-start.1 = (bf16[4,8,112,112]{3,2,1,0:T(8,128)(2,1)S(1)}, bf16[4,8,112,112]{3,2,1,0:T(8,128)(2,1)S(1)}, u32[]{:S(2)}, u32[]{:S(2)}) collective-permute-start(bf16[4,8,112,112]{3,2,1,0:T(8,128)(2,1)S(1)} %bitcast.13), channel_id=1, source_target_pairs={{0,1},{1,0},{2,3},{3,2},{4,5},{5,4},{6,7},{7,6},{8,9},{9,8},{10,11... | collective-permute-start | bytes 2408456 | tf_op jit(solution)/shard_map/ppermute | solution.py:47
  60.2 13.8 %all-to-all-start.1 = ((f32[8,8,128]{2,1,0:T(8,128)}), f32[8,8,128]{2,1,0:T(8,128)}, u32[]{:S(2)}, u32[]{:S(2)}) async-start(f32[8,8,128]{2,1,0:T(8,128)} %broadcast_in_dim.31), calls=%async_computation.1 | async-start | bytes 65536 | tf_op jit(solution)/shard_map/all_to_all | solution.py:26
  76.9 35.7 %all-to-all-start.2 = ((f16[8,112,448]{2,1,0:T(8,128)(2,1)}), f16[8,112,448]{2,1,0:T(8,128)(2,1)S(1)}, u32[]{:S(2)}, u32[]{:S(2)}) async-start(f16[8,112,448]{2,1,0:T(8,128)(2,1)} %multiply_convert_fusion), calls=%async_computation.2 | async-start | bytes 1835008 | tf_op jit(solution)/shard_map/all_to_all | solution.py:64
  87.8 25.0 %copy-start = (s32[56,56]{1,0:T(8,128)S(1)}, s32[56,56]{1,0:T(8,128)}, u32[]{:S(2)}) copy-start(s32[56,56]{1,0:T(8,128)} %param.7) | copy-start | bytes 37636
  87.8 25.0 %copy-start.2 = (s32[448]{0:T(512)S(1)}, s32[448]{0:T(512)}, u32[]{:S(2)}) copy-start(s32[448]{0:T(512)} %copy-done.1) | copy-start | bytes 5380
  87.8 25.0 %copy-start.4 = (s32[448]{0:T(512)S(1)}, s32[448]{0:T(512)}, u32[]{:S(2)}) copy-start(s32[448]{0:T(512)} %copy-done.3) | copy-start | bytes 5380
  87.8 25.0 %copy-start.7 = (pred[448]{0:T(512)(128)(4,1)S(1)}, pred[448]{0:T(512)(128)(4,1)}, u32[]{:S(2)}) copy-start(pred[448]{0:T(512)(128)(4,1)} %copy-done.6) | copy-start | bytes 1348
  87.8 25.5 %copy-start.5 = (f32[448]{0:T(512)S(1)}, f32[448]{0:T(512)}, u32[]{:S(2)}) copy-start(f32[448]{0:T(512)} %get-tuple-element.13) | copy-start | bytes 5380

commit v5 on v2

--- a/solution.py
+++ b/solution.py
@@ -3,6 +3,7 @@
 from jax import lax
 from jax.sharding import Mesh
 from jax.sharding import PartitionSpec as P
+
 
 BLK = 128
 F32 = jnp.float32
@@ -33,8 +34,8 @@
     in_mask = local_mask(in_pattern, row_start, rows, col_start, cols)
     masked = jnp.where(in_mask, similarity, jnp.zeros_like(similarity))
     half = rows // 2
+    front = y < n // 2
     low, high = masked[:half], masked[half:]
-    front = y < n // 2
     first = lax.ppermute(
         jnp.where(front, low, high), "y", [(i, 2 * i) if i < n // 2 else (i, 2 * i - n + 1) for i in range(n)]
     )
@@ -45,11 +46,12 @@
     left = jnp.broadcast_to(masked.T.reshape(n, 1, half, rows), (n, n, half, rows))
     left = lax.all_to_all(left.reshape(n * n, half, rows), ("y", "z"), 0, 0)
     left = left.reshape(n, cols, rows)
+    right_all = lax.all_gather(jnp.concatenate([first, second]), "x")
+    left, right_all = lax.optimization_barrier((left, right_all))
     part = jnp.sum(left.astype(F32), axis=(0, 2))
     part = jnp.concatenate([part, jnp.zeros((512 - cols,), F32)]).reshape(1, 4, 128)
     in_sums = lax.all_to_all(jnp.broadcast_to(part, (n, 4, 128)), "x", 0, 0)
     in_sums = jnp.sum(in_sums, axis=0).reshape(512)[:cols]
-    right_all = lax.all_gather(jnp.concatenate([first, second]), "x")
     left_own = (left.astype(F32) / in_sums[None, :, None]).astype(BF16)
     left_other = lax.ppermute(left_own, "core", [(0, 1), (1, 0)])
     slot = (core + y) % 2
@@ -78,6 +80,5 @@
 def solution(mesh):
     fine = Mesh(mesh.devices.reshape(8, 8, 8, 2), ("x", "y", "z", "core"))
     cells = P(("x", "y"), ("z", "core"))
-    return jax.shard_map(
-        body, mesh=fine, in_specs=(cells, P(), P()), out_specs=cells, check_vma=False
-    )
+
+    return jax.shard_map(body, mesh=fine, in_specs=(cells, P(), P()), out_specs=cells, check_vma=False)

time: 154 us -> 153 us (level)
  blocking collectives: 76.4 us -> 89.9 us
  starting transfers between devices: 39.5 us -> 32.2 us
  waiting for transfers between devices: 28.1 us -> 23.6 us
  local copies, waits for them, and re-layouts: 3.35 us -> 1.81 us
    all_to_all x0 -> x1, blocking collectives: none -> 13.6 us  [body(): in_sums = lax.all_to_all(jnp.broadcast_to(part, (n, 4, 128)), 'x', 0, 0)]
    all_to_all x1 -> x0, starting transfers between devices: 7.31 us -> none  [body(): in_sums = lax.all_to_all(jnp.broadcast_to(part, (n, 4, 128)), 'x', 0, 0)]
    all_to_all x1 -> x0, waiting for transfers between devices: 5.01 us -> none  [body(): in_sums = lax.all_to_all(jnp.broadcast_to(part, (n, 4, 128)), 'x', 0, 0)]
  transfers between devices with their start and end apart: 5 -> 4, of which waited for: 3 -> 2; matrix products, arithmetic and copies ran while one was open for 2% -> 0% of each run, Pallas kernels for 0% -> 0%
where the time goes in v5:
time: 153 us; the launch traced here: 152 us
  blocking collectives  89.9 us (59%)
  starting transfers between devices  32.2 us (21%)
  waiting for transfers between devices  23.6 us (15%)
  matrix products  3.18 us (2%)
  local copies, waits for them, and re-layouts  1.81 us (1%)
    all_to_all x1, blocking collectives, body(): partials = lax.all_to_all(partial, 'y', 0, 0)  28.9 us
    all_gather x1, blocking collectives, body(): right_all = lax.all_gather(jnp.concatenate([first, second]), 'x')  26.7 us
    all_to_all x1, starting transfers between devices, body(): left = lax.all_to_all(left.reshape(n * n, half, rows), ('y', 'z'), 0, 0)  23.4 us
    ppermute x1, waiting for transfers between devices, body(): lax.ppermute(jnp.where(front, high, low), 'y', [(i, 2 * i + 1) if i < n /...  21.9 us
    all_to_all x2, blocking collectives, body(): lax.all_to_all(jnp.broadcast_to(sums, (n, 8, 128)), axis, 0, 0)  20.7 us
    all_to_all x1, blocking collectives, body(): in_sums = lax.all_to_all(jnp.broadcast_to(part, (n, 4, 128)), 'x', 0, 0)  13.6 us
    ppermute x1, starting transfers between devices, body(): lax.ppermute(jnp.where(front, high, low), 'y', [(i, 2 * i + 1) if i < n /...  6.19 us
  transfers between devices with their start and end apart: 4, of which 2 were waited for; matrix products, arithmetic and copies ran while one was open for 0% of the time, Pallas kernels for 0%

profile of v5, /device:TPU:2, one launch (start us, length us, event | category | flops | bytes accessed | tf_op | source)
XLA Modules:
  0.0 152.4 jit_solution(5632530642260874651)
XLA Ops:
  0.1 1.4 convert_reduce_fusion.2
  1.5 0.1 copy.15
  1.6 1.1 broadcast_in_dim.36
  2.7 23.4 %all-to-all-start = ((bf16[64,56,112]{2,1,0:T(8,128)(2,1)}), bf16[64,56,112]{2,1,0:T(8,128)(2,1)S(1)}, u32[]{:S(2)}, u32[]{:S(2)}) async-start(bf16[64,56,112]{2,1,0:T(8,128)(2,1)} %bitcast.2), calls=%async_computation | async-start | bytes 1835008 | tf_op jit(solution)/shard_map/all_to_all | solution.py:47
  26.1 0.7 collective-permute-start
  26.8 6.2 %collective-permute-start.1 = (bf16[56,448]{1,0:T(8,128)(2,1)S(1)}, bf16[56,448]{1,0:T(8,128)(2,1)S(1)}, u32[]{:S(2)}, u32[]{:S(2)}) collective-permute-start(bf16[56,448]{1,0:T(8,128)(2,1)S(1)} %get-tuple-element.12), channel_id=1, source_target_pairs={{0,16},{16,48},{32,80},{48,112},{64,0},{80,32},{96,64},{112,96},{1... | collective-permute-start | bytes 150536 | tf_op jit(solution)/shard_map/ppermute | solution.py:42
  33.0 0.0 collective-permute-done
  33.0 21.9 %collective-permute-done.1 = bf16[56,448]{1,0:T(8,128)(2,1)S(1)} collective-permute-done((bf16[56,448]{1,0:T(8,128)(2,1)S(1)}, bf16[56,448]{1,0:T(8,128)(2,1)S(1)}, u32[]{:S(2)}, u32[]{:S(2)}) %collective-permute-start.1) | collective-permute-done | bytes 50208 | tf_op jit(solution)/shard_map/ppermute | solution.py:42
  55.0 26.7 %all-gather = bf16[896,448]{1,0:T(8,128)(2,1)S(1)} all-gather(bf16[112,448]{1,0:T(8,128)(2,1)S(1)} %pad_maximum_fusion), channel_id=2, replica_groups=mesh['x'=8,'y'=8,'z'=8,'core'=2] {'x'}, dimensions={0}, use_global_device_ids=true | all-gather | bytes 903168 | tf_op jit(solution)/shard_map/all_gather | solution.py:49
  81.7 0.0 all-to-all-done
  81.7 0.5 copy.16
  82.2 0.2 convert_reduce_fusion
  82.4 13.6 %all_to_all.25 = f32[8,4,128]{2,1,0:T(4,128)S(1)} all-to-all(f32[8,4,128]{2,1,0:T(4,128)S(1)} %broadcast_in_dim.38), channel_id=1, replica_groups=mesh['x'=8,'y'=8,'z'=8,'core'=2] {'x'}, dimensions={0} | all-to-all | bytes 32768 | tf_op jit(solution)/shard_map/all_to_all | solution.py:53
  96.0 0.2 fusion
  96.2 1.9 %collective-permute-start.2 = (bf16[8,448,112]{1,2,0:T(8,128)(2,1)S(1)}, bf16[8,448,112]{1,2,0:T(8,128)(2,1)S(1)}, u32[]{:S(2)}, u32[]{:S(2)}) collective-permute-start(bf16[8,448,112]{1,2,0:T(8,128)(2,1)S(1)} %fusion), channel_id=1, source_target_pairs={{0,1},{1,0},{2,3},{3,2},{4,5},{5,4},{6,7},{7,6},{8,9},{9,8},{10,11... | collective-permute-start | bytes 2408456 | tf_op jit(solution)/shard_map/ppermute | solution.py:56
  98.1 0.1 constant_dynamic-slice_fusion
  98.2 0.6 fusion.34
  98.9 1.7 %collective-permute-done.2 = bf16[8,448,112]{1,2,0:T(8,128)(2,1)S(1)} collective-permute-done((bf16[8,448,112]{1,2,0:T(8,128)(2,1)S(1)}, bf16[8,448,112]{1,2,0:T(8,128)(2,1)S(1)}, u32[]{:S(2)}, u32[]{:S(2)}) %collective-permute-start.2) | collective-permute-done | bytes 802848 | tf_op jit(solution)/shard_map/ppermute | solution.py:56
  100.6 0.6 multiply_convert_fusion
  101.2 0.0 copy-start
  101.2 28.9 %all_to_all.26 = f16[8,112,448]{2,1,0:T(8,128)(2,1)S(1)} all-to-all(f16[8,112,448]{2,1,0:T(8,128)(2,1)S(1)} %multiply_convert_fusion), channel_id=1, replica_groups=mesh['x'=8,'y'=8,'z'=8,'core'=2] {'y'}, dimensions={0} | all-to-all | bytes 1605632 | tf_op jit(solution)/shard_map/all_to_all | solution.py:65
  130.1 0.1 convert_reduce_fusion.1
  130.3 0.0 copy-done
  130.3 0.5 multiply_reduce_fusion
  130.8 0.1 maximum_bitcast_fusion
  130.9 10.4 %all_to_all.27 = f32[8,8,128]{2,1,0:T(8,128)S(1)} all-to-all(f32[8,8,128]{2,1,0:T(8,128)S(1)} %broadcast_in_dim.41), channel_id=1, replica_groups=mesh['x'=8,'y'=8,'z'=8,'core'=2] {'y'}, dimensions={0} | all-to-all | bytes 65536 | tf_op jit(solution)/shard_map/all_to_all | solution.py:72
  141.3 10.3 %all_to_all.28 = f32[8,8,128]{2,1,0:T(8,128)S(1)} all-to-all(f32[8,8,128]{2,1,0:T(8,128)S(1)} %broadcast_in_dim.42), channel_id=1, replica_groups=mesh['x'=8,'y'=8,'z'=8,'core'=2] {'x'}, dimensions={0} | all-to-all | bytes 65536 | tf_op jit(solution)/shard_map/all_to_all | solution.py:72
  151.6 0.1 fusion.29
  151.7 0.7 divide_convert_fusion
  (14 shorter events, 0.1 us)
Async XLA Ops:
  2.7 79.0 %all-to-all-start = ((bf16[64,56,112]{2,1,0:T(8,128)(2,1)}), bf16[64,56,112]{2,1,0:T(8,128)(2,1)S(1)}, u32[]{:S(2)}, u32[]{:S(2)}) async-start(bf16[64,56,112]{2,1,0:T(8,128)(2,1)} %bitcast.2), calls=%async_computation | async-start | bytes 1835008 | tf_op jit(solution)/shard_map/all_to_all | solution.py:47
  26.1 6.9 %collective-permute-start = (bf16[56,448]{1,0:T(8,128)(2,1)S(1)}, bf16[56,448]{1,0:T(8,128)(2,1)S(1)}, u32[]{:S(2)}, u32[]{:S(2)}) collective-permute-start(bf16[56,448]{1,0:T(8,128)(2,1)S(1)} %get-tuple-element.11), channel_id=1, source_target_pairs={{0,0},{16,32},{32,64},{48,96},{64,16},{80,48},{96,80},{112,112},{1... | collective-permute-start | bytes 150536 | tf_op jit(solution)/shard_map/ppermute | solution.py:39
  26.8 28.1 %collective-permute-start.1 = (bf16[56,448]{1,0:T(8,128)(2,1)S(1)}, bf16[56,448]{1,0:T(8,128)(2,1)S(1)}, u32[]{:S(2)}, u32[]{:S(2)}) collective-permute-start(bf16[56,448]{1,0:T(8,128)(2,1)S(1)} %get-tuple-element.12), channel_id=1, source_target_pairs={{0,16},{16,48},{32,80},{48,112},{64,0},{80,32},{96,64},{112,96},{1... | collective-permute-start | bytes 150536 | tf_op jit(solution)/shard_map/ppermute | solution.py:42
  96.2 4.4 %collective-permute-start.2 = (bf16[8,448,112]{1,2,0:T(8,128)(2,1)S(1)}, bf16[8,448,112]{1,2,0:T(8,128)(2,1)S(1)}, u32[]{:S(2)}, u32[]{:S(2)}) collective-permute-start(bf16[8,448,112]{1,2,0:T(8,128)(2,1)S(1)} %fusion), channel_id=1, source_target_pairs={{0,1},{1,0},{2,3},{3,2},{4,5},{5,4},{6,7},{7,6},{8,9},{9,8},{10,11... | collective-permute-start | bytes 2408456 | tf_op jit(solution)/shard_map/ppermute | solution.py:56
  101.2 29.1 %copy-start = (s32[56,56]{1,0:T(8,128)S(1)}, s32[56,56]{1,0:T(8,128)}, u32[]{:S(2)}) copy-start(s32[56,56]{1,0:T(8,128)} %param.5) | copy-start | bytes 37636

commit v6 on v5

--- a/solution.py
+++ b/solution.py
@@ -23,6 +23,13 @@
     return jnp.dot(by_row, pick_col, preferred_element_type=F32) > 0.5
 
 
+def split3(v):
+    hi = v.astype(BF16)
+    rest = v - hi.astype(F32)
+    mid = rest.astype(BF16)
+    return hi, mid, (rest - mid.astype(F32)).astype(BF16)
+
+
 def body(similarity, in_pattern, out_pattern):
     rows, cols = similarity.shape
     x, y = lax.axis_index("x"), lax.axis_index("y")
@@ -43,16 +50,17 @@
         jnp.where(front, high, low), "y", [(i, 2 * i + 1) if i < n // 2 else (i, 2 * i - n) for i in range(n)]
     )
     own_sums = jnp.sum(masked.astype(F32), axis=0)
-    left = jnp.broadcast_to(masked.T.reshape(n, 1, half, rows), (n, n, half, rows))
-    left = lax.all_to_all(left.reshape(n * n, half, rows), ("y", "z"), 0, 0)
-    left = left.reshape(n, cols, rows)
+    part = jnp.concatenate([own_sums, jnp.zeros((512 - cols,), F32)]).reshape(1, 4, 128)
+    part = lax.all_to_all(jnp.broadcast_to(part, (n, 4, 128)), "x", 0, 0)
+    part = jnp.sum(part, axis=0).reshape(1, 512)[:, :cols]
+    left = jnp.concatenate([masked, *split3(part), jnp.zeros((128 - rows - 3, cols), BF16)])
+    left = jnp.broadcast_to(left.T.reshape(n, 1, half, 128), (n, n, half, 128))
+    left = lax.all_to_all(left.reshape(n * n, half, 128), ("y", "z"), 0, 0)
+    left = left.reshape(n, cols, 128)
     right_all = lax.all_gather(jnp.concatenate([first, second]), "x")
     left, right_all = lax.optimization_barrier((left, right_all))
-    part = jnp.sum(left.astype(F32), axis=(0, 2))
-    part = jnp.concatenate([part, jnp.zeros((512 - cols,), F32)]).reshape(1, 4, 128)
-    in_sums = lax.all_to_all(jnp.broadcast_to(part, (n, 4, 128)), "x", 0, 0)
-    in_sums = jnp.sum(in_sums, axis=0).reshape(512)[:cols]
-    left_own = (left.astype(F32) / in_sums[None, :, None]).astype(BF16)
+    in_sums = jnp.sum(jnp.sum(left[:, :, rows : rows + 3].astype(F32), axis=0), axis=1, keepdims=True)
+    left_own = (left[:, :, :rows].astype(F32) / in_sums[None]).astype(BF16)
     left_other = lax.ppermute(left_own, "core", [(0, 1), (1, 0)])
     slot = (core + y) % 2
     halves = right_all.reshape(n, 2, half, cols)

time: 153 us -> 153 us (level)
  starting transfers between devices: 32.2 us -> 23.8 us
  blocking collectives: 89.9 us -> 98.2 us
  waiting for transfers between devices: 23.6 us -> 21.7 us
    all_to_all x1, starting transfers between devices: 23.4 us -> 15 us  [body(): left = lax.all_to_all(left.reshape(n * n, half, 128), ('y', 'z'), 0, 0)]
    all_to_all x1, blocking collectives: 13.6 us -> 21.9 us  [body(): part = lax.all_to_all(jnp.broadcast_to(part, (n, 4, 128)), 'x', 0, 0)]
    ppermute x1, waiting for transfers between devices: 21.9 us -> 19.9 us  [body(): lax.ppermute(jnp.where(front, high, low), 'y', [(i, 2 * i + 1) if i < n /...]
where the time goes in v6:
time: 153 us; the launch traced here: 152 us
  blocking collectives  98.2 us (64%)
  starting transfers between devices  23.8 us (16%)
  waiting for transfers between devices  21.7 us (14%)
  matrix products  4.36 us (3%)
  local copies, waits for them, and re-layouts  2 us (1%)
  other arithmetic  1.75 us (1%)
    all_to_all x1, blocking collectives, body(): partials = lax.all_to_all(partial, 'y', 0, 0)  28.9 us
    all_gather x1, blocking collectives, body(): right_all = lax.all_gather(jnp.concatenate([first, second]), 'x')  25.5 us
    all_to_all x2, blocking collectives, body(): lax.all_to_all(jnp.broadcast_to(sums, (n, 8, 128)), axis, 0, 0)  21.9 us
    all_to_all x1, blocking collectives, body(): part = lax.all_to_all(jnp.broadcast_to(part, (n, 4, 128)), 'x', 0, 0)  21.9 us
    ppermute x1, waiting for transfers between devices, body(): lax.ppermute(jnp.where(front, high, low), 'y', [(i, 2 * i + 1) if i < n /...  19.9 us
    all_to_all x1, starting transfers between devices, body(): left = lax.all_to_all(left.reshape(n * n, half, 128), ('y', 'z'), 0, 0)  15 us
    ppermute x1, starting transfers between devices, body(): lax.ppermute(jnp.where(front, high, low), 'y', [(i, 2 * i + 1) if i < n /...  6.19 us
  transfers between devices with their start and end apart: 4, of which 2 were waited for; matrix products, arithmetic and copies ran while one was open for 0% of the time, Pallas kernels for 0%

profile of v6, /device:TPU:2, one launch (start us, length us, event | category | flops | bytes accessed | tf_op | source)
XLA Modules:
  0.0 152.0 jit_solution(15380885091461740361)
XLA Ops:
  0.1 1.4 convert_reduce_fusion.2
  1.5 21.9 %all_to_all.25 = f32[8,4,128]{2,1,0:T(4,128)S(1)} all-to-all(f32[8,4,128]{2,1,0:T(4,128)S(1)} %broadcast_in_dim.38), channel_id=1, replica_groups=mesh['x'=8,'y'=8,'z'=8,'core'=2] {'x'}, dimensions={0} | all-to-all | bytes 32768 | tf_op jit(solution)/shard_map/all_to_all | solution.py:54
  23.4 0.2 concatenate.13
  23.6 0.1 copy.16
  23.7 1.1 broadcast_in_dim.41
  24.8 15.0 %all-to-all-start.1 = ((bf16[64,56,128]{2,1,0:T(8,128)(2,1)}), bf16[64,56,128]{2,1,0:T(8,128)(2,1)S(1)}, u32[]{:S(2)}, u32[]{:S(2)}) async-start(bf16[64,56,128]{2,1,0:T(8,128)(2,1)} %bitcast.4), calls=%async_computation.1 | async-start | bytes 1835008 | tf_op jit(solution)/shard_map/all_to_all | solution.py:58
  39.8 0.7 collective-permute-start
  40.5 6.2 %collective-permute-start.1 = (bf16[56,448]{1,0:T(8,128)(2,1)S(1)}, bf16[56,448]{1,0:T(8,128)(2,1)S(1)}, u32[]{:S(2)}, u32[]{:S(2)}) collective-permute-start(bf16[56,448]{1,0:T(8,128)(2,1)S(1)} %get-tuple-element.12), channel_id=1, source_target_pairs={{0,16},{16,48},{32,80},{48,112},{64,0},{80,32},{96,64},{112,96},{1... | collective-permute-start | bytes 150536 | tf_op jit(solution)/shard_map/ppermute | solution.py:49
  46.7 0.0 collective-permute-done
  46.7 19.9 %collective-permute-done.1 = bf16[56,448]{1,0:T(8,128)(2,1)S(1)} collective-permute-done((bf16[56,448]{1,0:T(8,128)(2,1)S(1)}, bf16[56,448]{1,0:T(8,128)(2,1)S(1)}, u32[]{:S(2)}, u32[]{:S(2)}) %collective-permute-start.1) | collective-permute-done | bytes 50208 | tf_op jit(solution)/shard_map/ppermute | solution.py:49
  66.6 25.5 %all-gather = bf16[896,448]{1,0:T(8,128)(2,1)S(1)} all-gather(bf16[112,448]{1,0:T(8,128)(2,1)S(1)} %pad_maximum_fusion), channel_id=2, replica_groups=mesh['x'=8,'y'=8,'z'=8,'core'=2] {'x'}, dimensions={0}, use_global_device_ids=true | all-gather | bytes 903168 | tf_op jit(solution)/shard_map/all_gather | solution.py:60
  92.1 0.0 all-to-all-done.1
  92.1 0.5 copy.17
  92.6 0.4 convert_reduce_fusion.1
  93.0 0.2 divide_convert_fusion
  93.2 1.9 %collective-permute-start.2 = (bf16[8,448,112]{1,2,0:T(8,128)(2,1)S(1)}, bf16[8,448,112]{1,2,0:T(8,128)(2,1)}, u32[]{:S(2)}, u32[]{:S(2)}) collective-permute-start(bf16[8,448,112]{1,2,0:T(8,128)(2,1)S(1)} %divide_convert_fusion), channel_id=1, source_target_pairs={{0,1},{1,0},{2,3},{3,2},{4,5},{5,4},{6,7},{7,6},{8,9},{9,8},{10,11... | collective-permute-start | bytes 2408456 | tf_op jit(solution)/shard_map/ppermute | solution.py:64
  95.2 0.1 constant_dynamic-slice_fusion
  95.3 0.6 fusion.34
  95.9 1.8 %collective-permute-done.2 = bf16[8,448,112]{1,2,0:T(8,128)(2,1)} collective-permute-done((bf16[8,448,112]{1,2,0:T(8,128)(2,1)S(1)}, bf16[8,448,112]{1,2,0:T(8,128)(2,1)}, u32[]{:S(2)}, u32[]{:S(2)}) %collective-permute-start.2) | collective-permute-done | bytes 802848 | tf_op jit(solution)/shard_map/ppermute | solution.py:64
  97.7 1.8 %multiply_convert_fusion = f16[8,112,448]{2,1,0:T(8,128)(2,1)S(1)} fusion(f32[8,112,448]{2,1,0:T(8,128)S(1)} %fusion.34, bf16[8,448,112]{1,2,0:T(8,128)(2,1)} %collective-permute-done.2, bf16[448,448,1]{1,0,2:T(8,128)(2,1)S(1)} %bitcast.30), kind=kOutput, calls=%fused_computation.1 | convolution fusion | flops 360865792 | bytes 3612672 | tf_op jit(solution)/shard_map/dot_general | solution.py:71
  99.5 0.0 copy-start
  99.6 28.9 %all_to_all.26 = f16[8,112,448]{2,1,0:T(8,128)(2,1)S(1)} all-to-all(f16[8,112,448]{2,1,0:T(8,128)(2,1)S(1)} %multiply_convert_fusion), channel_id=1, replica_groups=mesh['x'=8,'y'=8,'z'=8,'core'=2] {'y'}, dimensions={0} | all-to-all | bytes 1605632 | tf_op jit(solution)/shard_map/all_to_all | solution.py:73
  128.5 0.1 convert_reduce_fusion
  128.6 0.0 copy-done
  128.6 0.5 multiply_reduce_fusion
  129.1 0.1 maximum_bitcast_fusion
  129.2 10.4 %all_to_all.27 = f32[8,8,128]{2,1,0:T(8,128)S(1)} all-to-all(f32[8,8,128]{2,1,0:T(8,128)S(1)} %broadcast_in_dim.44), channel_id=1, replica_groups=mesh['x'=8,'y'=8,'z'=8,'core'=2] {'y'}, dimensions={0} | all-to-all | bytes 65536 | tf_op jit(solution)/shard_map/all_to_all | solution.py:80
  139.6 11.6 %all_to_all.28 = f32[8,8,128]{2,1,0:T(8,128)S(1)} all-to-all(f32[8,8,128]{2,1,0:T(8,128)S(1)} %broadcast_in_dim.45), channel_id=1, replica_groups=mesh['x'=8,'y'=8,'z'=8,'core'=2] {'x'}, dimensions={0} | all-to-all | bytes 65536 | tf_op jit(solution)/shard_map/all_to_all | solution.py:80
  151.2 0.1 fusion.29
  151.3 0.7 divide_convert_fusion.1
  (17 shorter events, 0.2 us)
Async XLA Ops:
  24.8 67.3 %all-to-all-start.1 = ((bf16[64,56,128]{2,1,0:T(8,128)(2,1)}), bf16[64,56,128]{2,1,0:T(8,128)(2,1)S(1)}, u32[]{:S(2)}, u32[]{:S(2)}) async-start(bf16[64,56,128]{2,1,0:T(8,128)(2,1)} %bitcast.4), calls=%async_computation.1 | async-start | bytes 1835008 | tf_op jit(solution)/shard_map/all_to_all | solution.py:58
  39.8 6.9 %collective-permute-start = (bf16[56,448]{1,0:T(8,128)(2,1)S(1)}, bf16[56,448]{1,0:T(8,128)(2,1)S(1)}, u32[]{:S(2)}, u32[]{:S(2)}) collective-permute-start(bf16[56,448]{1,0:T(8,128)(2,1)S(1)} %get-tuple-element.11), channel_id=1, source_target_pairs={{0,0},{16,32},{32,64},{48,96},{64,16},{80,48},{96,80},{112,112},{1... | collective-permute-start | bytes 150536 | tf_op jit(solution)/shard_map/ppermute | solution.py:46
  40.5 26.1 %collective-permute-start.1 = (bf16[56,448]{1,0:T(8,128)(2,1)S(1)}, bf16[56,448]{1,0:T(8,128)(2,1)S(1)}, u32[]{:S(2)}, u32[]{:S(2)}) collective-permute-start(bf16[56,448]{1,0:T(8,128)(2,1)S(1)} %get-tuple-element.12), channel_id=1, source_target_pairs={{0,16},{16,48},{32,80},{48,112},{64,0},{80,32},{96,64},{112,96},{1... | collective-permute-start | bytes 150536 | tf_op jit(solution)/shard_map/ppermute | solution.py:49
  93.2 4.5 %collective-permute-start.2 = (bf16[8,448,112]{1,2,0:T(8,128)(2,1)S(1)}, bf16[8,448,112]{1,2,0:T(8,128)(2,1)}, u32[]{:S(2)}, u32[]{:S(2)}) collective-permute-start(bf16[8,448,112]{1,2,0:T(8,128)(2,1)S(1)} %divide_convert_fusion), channel_id=1, source_target_pairs={{0,1},{1,0},{2,3},{3,2},{4,5},{5,4},{6,7},{7,6},{8,9},{9,8},{10,11... | collective-permute-start | bytes 2408456 | tf_op jit(solution)/shard_map/ppermute | solution.py:64
  99.5 29.1 %copy-start = (s32[56,56]{1,0:T(8,128)S(1)}, s32[56,56]{1,0:T(8,128)}, u32[]{:S(2)}) copy-start(s32[56,56]{1,0:T(8,128)} %param.5) | copy-start | bytes 37636

commit v7 on v2

--- a/solution.py
+++ b/solution.py
@@ -3,6 +3,7 @@
 from jax import lax
 from jax.sharding import Mesh
 from jax.sharding import PartitionSpec as P
+
 
 BLK = 128
 F32 = jnp.float32
@@ -32,30 +33,27 @@
     col_start = (z * 2 + core) * cols
     in_mask = local_mask(in_pattern, row_start, rows, col_start, cols)
     masked = jnp.where(in_mask, similarity, jnp.zeros_like(similarity))
+    own_sums = jnp.sum(masked.astype(F32), axis=0)
     half = rows // 2
-    low, high = masked[:half], masked[half:]
-    front = y < n // 2
-    first = lax.ppermute(
-        jnp.where(front, low, high), "y", [(i, 2 * i) if i < n // 2 else (i, 2 * i - n + 1) for i in range(n)]
-    )
-    second = lax.ppermute(
-        jnp.where(front, high, low), "y", [(i, 2 * i + 1) if i < n // 2 else (i, 2 * i - n) for i in range(n)]
-    )
-    own_sums = jnp.sum(masked.astype(F32), axis=0)
-    left = jnp.broadcast_to(masked.T.reshape(n, 1, half, rows), (n, n, half, rows))
+    blocks = masked.T.reshape(n // 2, 2, half, rows)
+    keep = jnp.where(core == 0, blocks[:, 0], blocks[:, 1])
+    give = jnp.where(core == 0, blocks[:, 1], blocks[:, 0])
+    got = lax.ppermute(give, "core", [(0, 1), (1, 0)])
+    left = jnp.where(core == 0, jnp.concatenate([keep, got]), jnp.concatenate([got, keep]))
+    left = jnp.broadcast_to(left[:, None], (n, n, half, rows))
     left = lax.all_to_all(left.reshape(n * n, half, rows), ("y", "z"), 0, 0)
     left = left.reshape(n, cols, rows)
+    right_all = lax.all_gather(masked, "x", tiled=True)
+    left, right_all = lax.optimization_barrier((left, right_all))
     part = jnp.sum(left.astype(F32), axis=(0, 2))
     part = jnp.concatenate([part, jnp.zeros((512 - cols,), F32)]).reshape(1, 4, 128)
     in_sums = lax.all_to_all(jnp.broadcast_to(part, (n, 4, 128)), "x", 0, 0)
     in_sums = jnp.sum(in_sums, axis=0).reshape(512)[:cols]
-    right_all = lax.all_gather(jnp.concatenate([first, second]), "x")
     left_own = (left.astype(F32) / in_sums[None, :, None]).astype(BF16)
     left_other = lax.ppermute(left_own, "core", [(0, 1), (1, 0)])
-    slot = (core + y) % 2
     halves = right_all.reshape(n, 2, half, cols)
-    right_own = lax.dynamic_index_in_dim(halves, slot, 1, False).reshape(cols, cols)
-    right_other = lax.dynamic_index_in_dim(halves, 1 - slot, 1, False).reshape(cols, cols)
+    right_own = lax.dynamic_index_in_dim(halves, core, 1, False).reshape(cols, cols)
+    right_other = lax.dynamic_index_in_dim(halves, 1 - core, 1, False).reshape(cols, cols)
     over_k = (((1,), (0,)), ((), ()))
     partial = lax.dot_general(left_own, right_own, over_k, preferred_element_type=F32)
     partial = partial + lax.dot_general(left_other, right_other, over_k, preferred_element_type=F32)
@@ -78,6 +76,7 @@
 def solution(mesh):
     fine = Mesh(mesh.devices.reshape(8, 8, 8, 2), ("x", "y", "z", "core"))
     cells = P(("x", "y"), ("z", "core"))
+
     return jax.shard_map(
         body, mesh=fine, in_specs=(cells, P(), P()), out_specs=cells, check_vma=False
     )

time: 154 us -> 131 us (0.85)
  waiting for transfers between devices: 28.1 us -> 2.93 us
  blocking collectives: 76.4 us -> 93.5 us
  starting transfers between devices: 39.5 us -> 27.2 us
  local copies, waits for them, and re-layouts: 3.35 us -> 1.8 us
    ppermute x2 -> x1, waiting for transfers between devices: 21.9 us -> 1.21 us  [body(): got = lax.ppermute(give, 'core', [(0, 1), (1, 0)])]
    all_to_all x0 -> x1, blocking collectives: none -> 13.4 us  [body(): in_sums = lax.all_to_all(jnp.broadcast_to(part, (n, 4, 128)), 'x', 0, 0)]
    all_to_all x1 -> x0, starting transfers between devices: 7.31 us -> none  [body(): in_sums = lax.all_to_all(jnp.broadcast_to(part, (n, 4, 128)), 'x', 0, 0)]
    all_to_all x1 -> x0, waiting for transfers between devices: 5.01 us -> none  [body(): in_sums = lax.all_to_all(jnp.broadcast_to(part, (n, 4, 128)), 'x', 0, 0)]
    ppermute x2 -> x1, starting transfers between devices: 6.86 us -> 1.92 us  [body(): got = lax.ppermute(give, 'core', [(0, 1), (1, 0)])]
    all_to_all x1, blocking collectives: 28.9 us -> 32.8 us  [body(): partials = lax.all_to_all(partial, 'y', 0, 0)]
  transfers between devices with their start and end apart: 5 -> 3, of which waited for: 3 -> 2; matrix products, arithmetic and copies ran while one was open for 2% -> 1% of each run, Pallas kernels for 0% -> 0%
where the time goes in v7:
time: 131 us; the launch traced here: 130 us
  blocking collectives  93.5 us (71%)
  starting transfers between devices  27.2 us (21%)
  matrix products  3.18 us (2%)
  waiting for transfers between devices  2.93 us (2%)
  local copies, waits for them, and re-layouts  1.8 us (1%)
  other arithmetic  1.52 us (1%)
    all_to_all x1, blocking collectives, body(): partials = lax.all_to_all(partial, 'y', 0, 0)  32.8 us
    all_gather x1, blocking collectives, body(): right_all = lax.all_gather(masked, 'x', tiled=True)  26.6 us
    all_to_all x1, starting transfers between devices, body(): left = lax.all_to_all(left.reshape(n * n, half, rows), ('y', 'z'), 0, 0)  23.4 us
    all_to_all x2, blocking collectives, body(): lax.all_to_all(jnp.broadcast_to(sums, (n, 8, 128)), axis, 0, 0)  20.7 us
    all_to_all x1, blocking collectives, body(): in_sums = lax.all_to_all(jnp.broadcast_to(part, (n, 4, 128)), 'x', 0, 0)  13.4 us
  transfers between devices with their start and end apart: 3, of which 2 were waited for; matrix products, arithmetic and copies ran while one was open for 1% of the time, Pallas kernels for 0%

profile of v7, /device:TPU:2, one launch (start us, length us, event | category | flops | bytes accessed | tf_op | source)
XLA Modules:
  0.0 130.3 jit_solution(13946713007250543297)
XLA Ops:
  0.1 1.4 %convert_reduce_fusion.2 = (f32[448]{0:T(512)S(1)}, bf16[112,448]{1,0:T(8,128)(2,1)S(1)}) fusion(bf16[112,448]{1,0:T(8,128)(2,1)} %param.3, s32[448]{0:T(512)S(1)} %get-tuple-element.21, s32[448]{0:T(512)S(1)} %get-tuple-element.22, pred[448]{0:T(512)(128)(4,1)S(1)} %fusion.28, s32[112]{0:T(128)S(1)} %get-tuple-element.19, s32[112]{0:T(128)S(1)} %get-tuple-element.20, ...), kind=kOutput, calls=%fused_computation.11 | convolution fusion | flops 6603968 | bytes 220080 | tf_op jit(solution)/shard_map/dot_general | solution.py:23
  1.5 0.1 copy.13
  1.6 1.9 %collective-permute-start = (bf16[4,56,112]{2,1,0:T(8,128)(2,1)S(1)}, bf16[4,56,112]{2,1,0:T(8,128)(2,1)S(1)}, u32[]{:S(2)}, u32[]{:S(2)}) collective-permute-start(bf16[4,56,112]{2,1,0:T(8,128)(2,1)S(1)} %get-tuple-element.12), channel_id=1, source_target_pairs={{0,1},{1,0},{2,3},{3,2},{4,5},{5,4},{6,7},{7,6},{8,9},{9,8},{10,11... | collective-permute-start | bytes 150536 | tf_op jit(solution)/shard_map/ppermute | solution.py:41
  3.6 1.2 collective-permute-done
  4.8 1.0 broadcast_in_dim.34
  5.9 23.4 %all-to-all-start = ((bf16[64,56,112]{2,1,0:T(8,128)(2,1)}), bf16[64,56,112]{2,1,0:T(8,128)(2,1)S(1)}, u32[]{:S(2)}, u32[]{:S(2)}) async-start(bf16[64,56,112]{2,1,0:T(8,128)(2,1)} %bitcast.4), calls=%async_computation | async-start | bytes 1835008 | tf_op jit(solution)/shard_map/all_to_all | solution.py:44
  29.3 26.6 %all_gather.3 = bf16[896,448]{1,0:T(8,128)(2,1)S(1)} all-gather(bf16[112,448]{1,0:T(8,128)(2,1)S(1)} %get-tuple-element.16), channel_id=1, replica_groups=mesh['x'=8,'y'=8,'z'=8,'core'=2] {'x'}, dimensions={0}, use_global_device_ids=true | all-gather | bytes 903168 | tf_op jit(solution)/shard_map/all_gather | solution.py:46
  55.8 0.0 all-to-all-done
  55.8 0.5 copy.14
  56.4 0.2 convert_reduce_fusion
  56.6 13.4 %all_to_all.25 = f32[8,4,128]{2,1,0:T(4,128)S(1)} all-to-all(f32[8,4,128]{2,1,0:T(4,128)S(1)} %broadcast_in_dim.36), channel_id=1, replica_groups=mesh['x'=8,'y'=8,'z'=8,'core'=2] {'x'}, dimensions={0} | all-to-all | bytes 32768 | tf_op jit(solution)/shard_map/all_to_all | solution.py:50
  70.0 0.2 fusion
  70.2 1.9 %collective-permute-start.1 = (bf16[8,448,112]{1,2,0:T(8,128)(2,1)S(1)}, bf16[8,448,112]{1,2,0:T(8,128)(2,1)S(1)}, u32[]{:S(2)}, u32[]{:S(2)}) collective-permute-start(bf16[8,448,112]{1,2,0:T(8,128)(2,1)S(1)} %fusion), channel_id=1, source_target_pairs={{0,1},{1,0},{2,3},{3,2},{4,5},{5,4},{6,7},{7,6},{8,9},{9,8},{10,11... | collective-permute-start | bytes 2408456 | tf_op jit(solution)/shard_map/ppermute | solution.py:53
  72.1 0.1 constant_dynamic-slice_fusion
  72.2 0.6 fusion.34
  72.8 1.7 %collective-permute-done.1 = bf16[8,448,112]{1,2,0:T(8,128)(2,1)S(1)} collective-permute-done((bf16[8,448,112]{1,2,0:T(8,128)(2,1)S(1)}, bf16[8,448,112]{1,2,0:T(8,128)(2,1)S(1)}, u32[]{:S(2)}, u32[]{:S(2)}) %collective-permute-start.1) | collective-permute-done | bytes 802848 | tf_op jit(solution)/shard_map/ppermute | solution.py:53
  74.5 0.6 multiply_convert_fusion
  75.2 0.0 copy-start
  75.2 32.8 %all_to_all.26 = f16[8,112,448]{2,1,0:T(8,128)(2,1)S(1)} all-to-all(f16[8,112,448]{2,1,0:T(8,128)(2,1)S(1)} %multiply_convert_fusion), channel_id=1, replica_groups=mesh['x'=8,'y'=8,'z'=8,'core'=2] {'y'}, dimensions={0} | all-to-all | bytes 1605632 | tf_op jit(solution)/shard_map/all_to_all | solution.py:61
  108.0 0.1 convert_reduce_fusion.1
  108.1 0.0 copy-done
  108.1 0.5 multiply_reduce_fusion
  108.7 0.1 maximum_bitcast_fusion
  108.7 10.4 %all_to_all.27 = f32[8,8,128]{2,1,0:T(8,128)S(1)} all-to-all(f32[8,8,128]{2,1,0:T(8,128)S(1)} %broadcast_in_dim.39), channel_id=1, replica_groups=mesh['x'=8,'y'=8,'z'=8,'core'=2] {'y'}, dimensions={0} | all-to-all | bytes 65536 | tf_op jit(solution)/shard_map/all_to_all | solution.py:68
  119.1 10.3 %all_to_all.28 = f32[8,8,128]{2,1,0:T(8,128)S(1)} all-to-all(f32[8,8,128]{2,1,0:T(8,128)S(1)} %broadcast_in_dim.40), channel_id=1, replica_groups=mesh['x'=8,'y'=8,'z'=8,'core'=2] {'x'}, dimensions={0} | all-to-all | bytes 65536 | tf_op jit(solution)/shard_map/all_to_all | solution.py:68
  129.5 0.1 fusion.29
  129.6 0.7 divide_convert_fusion
  (14 shorter events, 0.2 us)
Async XLA Ops:
  1.6 3.1 %collective-permute-start = (bf16[4,56,112]{2,1,0:T(8,128)(2,1)S(1)}, bf16[4,56,112]{2,1,0:T(8,128)(2,1)S(1)}, u32[]{:S(2)}, u32[]{:S(2)}) collective-permute-start(bf16[4,56,112]{2,1,0:T(8,128)(2,1)S(1)} %get-tuple-element.12), channel_id=1, source_target_pairs={{0,1},{1,0},{2,3},{3,2},{4,5},{5,4},{6,7},{7,6},{8,9},{9,8},{10,11... | collective-permute-start | bytes 150536 | tf_op jit(solution)/shard_map/ppermute | solution.py:41
  5.9 50.0 %all-to-all-start = ((bf16[64,56,112]{2,1,0:T(8,128)(2,1)}), bf16[64,56,112]{2,1,0:T(8,128)(2,1)S(1)}, u32[]{:S(2)}, u32[]{:S(2)}) async-start(bf16[64,56,112]{2,1,0:T(8,128)(2,1)} %bitcast.4), calls=%async_computation | async-start | bytes 1835008 | tf_op jit(solution)/shard_map/all_to_all | solution.py:44
  70.2 4.4 %collective-permute-start.1 = (bf16[8,448,112]{1,2,0:T(8,128)(2,1)S(1)}, bf16[8,448,112]{1,2,0:T(8,128)(2,1)S(1)}, u32[]{:S(2)}, u32[]{:S(2)}) collective-permute-start(bf16[8,448,112]{1,2,0:T(8,128)(2,1)S(1)} %fusion), channel_id=1, source_target_pairs={{0,1},{1,0},{2,3},{3,2},{4,5},{5,4},{6,7},{7,6},{8,9},{9,8},{10,11... | collective-permute-start | bytes 2408456 | tf_op jit(solution)/shard_map/ppermute | solution.py:53
  75.2 33.0 %copy-start = (s32[56,56]{1,0:T(8,128)S(1)}, s32[56,56]{1,0:T(8,128)}, u32[]{:S(2)}) copy-start(s32[56,56]{1,0:T(8,128)} %param.5) | copy-start | bytes 37636

commit v8 on v3

v8 whole, which is shorter than its diff:
```python
import jax
import jax.numpy as jnp
from jax import lax
from jax.sharding import Mesh
from jax.sharding import PartitionSpec as P


BLK = 128
F32 = jnp.float32
BF16 = jnp.bfloat16
SCALE = 32.0

def local_mask(pattern, row_start, rows, col_start, cols):
    blocks = pattern.shape[0]
    row_blocks = (row_start + lax.broadcasted_iota(jnp.int32, (rows, blocks), 0)) // BLK
    pick_row = (row_blocks == lax.broadcasted_iota(jnp.int32, (rows, blocks), 1)).astype(BF16)
    col_blocks = (col_start + lax.broadcasted_iota(jnp.int32, (blocks, cols), 1)) // BLK
    pick_col = (col_blocks == lax.broadcasted_iota(jnp.int32, (blocks, cols), 0)).astype(BF16)
    eye = jnp.eye(blocks, dtype=jnp.int32)
    kept = jnp.maximum(pattern, eye).astype(BF16)
    by_row = jnp.dot(pick_row, kept, preferred_element_type=F32).astype(BF16)
    return jnp.dot(by_row, pick_col, preferred_element_type=F32) > 0.5

def send_all(v, axes, count):
    return jnp.sum(lax.all_to_all(jnp.broadcast_to(v, (count,) + v.shape), axes, 0, 0), axis=0)

def body(similarity, in_pattern, out_pattern):
    rows, cols = similarity.shape
    x, quad, spot = lax.axis_index("x"), lax.axis_index("quad"), lax.axis_index("spot")
    z, core = lax.axis_index("z"), lax.axis_index("core")
    n, m = lax.axis_size("x"), lax.axis_size("spot")
    order = rows * n * n
    row_start = (x * n + quad * m + spot) * rows
    col_start = (z * 2 + core) * cols
    swap = [(0, 1), (1, 0)]
    in_mask = local_mask(in_pattern, row_start, rows, col_start, cols)
    masked = jnp.where(in_mask, similarity, jnp.zeros_like(similarity))
    own_sums = jnp.sum(masked.astype(F32), axis=0)

    mine = masked.astype(jnp.float16)
    other = lax.ppermute(mine, "quad", swap)
    left = jnp.broadcast_to(masked.T.reshape(m, 1, rows, rows), (m, n, rows, rows))
    left = lax.all_to_all(left.reshape(m * n, rows, rows), ("spot", "z"), 0, 0)
    left = left.reshape(m, n, rows, rows)
    right = jnp.where(quad == 0, jnp.concatenate([mine, other]), jnp.concatenate([other, mine]))
    right = lax.all_gather(right, "x", tiled=True)
    left, right = lax.optimization_barrier((left, right))
    part = jnp.sum(left.astype(F32), axis=(0, 3))
    part = jnp.pad(part, ((0, 0), (0, 128 - rows)))
    in_sums = send_all(part, ("x", "quad"), 2 * n)[:, :rows, None]
    left_own = (left.astype(F32) / in_sums).astype(BF16)
    left_other = lax.ppermute(left_own, "core", swap)
    halves = right.reshape(n, 2, rows, cols)

    def times(l, which):
        r = lax.dynamic_index_in_dim(halves, which, 1, False).reshape(n * rows, cols).astype(BF16)
        l = l.reshape(m, n * rows, rows)
        return lax.dot_general(l, r, (((1,), (0,)), ((), ())), preferred_element_type=F32)

    partial = times(left_own, core) + times(left_other, 1 - core)
    partial = (partial * F32(SCALE)).astype(jnp.float16)
    partials = lax.all_to_all(partial, "spot", 0, 0)
    product = jnp.sum(partials.astype(F32), axis=0) * F32(1.0 / SCALE)
    out_mask = local_mask(out_pattern, row_start, rows, col_start, cols)
    product = jnp.where(out_mask, product, F32(0.0))
    sums = jnp.concatenate([jnp.sum(product * product, axis=0), own_sums, jnp.zeros((1024 - 2 * cols,), F32)])
    sums = send_all(send_all(sums.reshape(8, 128), ("quad", "spot"), n), "x", n).reshape(1024)
    own_in = sums[cols : 2 * cols]
    expanded = product / own_in
    out_sums = sums[:cols] / (own_in * own_in)
    return (F32(order) * (expanded * expanded) / out_sums).astype(BF16)

def solution(mesh):
    fine = Mesh(mesh.devices.reshape(8, 2, 4, 8, 2), ("x", "quad", "spot", "z", "core"))
    cells = P(("x", "quad", "spot"), ("z", "core"))

    return jax.shard_map(
        body, mesh=fine, in_specs=(cells, P(), P()), out_specs=cells, check_vma=False
    )
```

time: 134 us -> 146 us (1.090)
  waiting for transfers between devices: 6.51 us -> 29.4 us
  blocking collectives: 84.1 us -> 70.2 us
  starting transfers between devices: 34.6 us -> 36.6 us
  matrix products: 3.24 us -> 5.19 us
    all_to_all x1 -> x0, blocking collectives: 36.7 us -> none  [body(): partials = lax.all_to_all(partial, ('quad', 'spot'), 0, 0)]
    all_to_all x2 -> x3, blocking collectives: 20.9 us -> 40.9 us  [send_all(): lax.all_to_all(jnp.broadcast_to(v, (count,) + v.shape), axes, 0, 0)]
    ppermute x2, waiting for transfers between devices: 0.01 us -> 16.1 us  [the longest x1 15.7 us: body(): other = lax.ppermute(mine, 'quad', swap)]
    all_to_all x1, waiting for transfers between devices: 6.5 us -> 13.3 us  [body(): partials = lax.all_to_all(partial, 'spot', 0, 0)]
    all_gather x1, blocking collectives: 26.5 us -> 29.3 us  [body(): right = lax.all_gather(right, 'x', tiled=True)]
    dot_general x2, matrix products: 1.34 us -> 3.3 us  [times(): lax.dot_general(l, r, (((1,), (0,)), ((), ())), preferred_element_type=F32)]
    all_to_all x1, starting transfers between devices: 7.13 us -> 8.77 us  [body(): partials = lax.all_to_all(partial, 'spot', 0, 0)]
  transfers between devices with their start and end apart: 4 -> 4, of which waited for: 1 -> 3; matrix products, arithmetic and copies ran while one was open for 1% -> 2% of each run, Pallas kernels for 0% -> 0%
where the time goes in v8:
time: 146 us
  blocking collectives  70.2 us (48%)
  starting transfers between devices  36.6 us (25%)
  waiting for transfers between devices  29.4 us (20%)
  matrix products  5.19 us (4%)
  other arithmetic  2.97 us (2%)
    all_to_all x3, blocking collectives, send_all(): lax.all_to_all(jnp.broadcast_to(v, (count,) + v.shape), axes, 0, 0)  40.9 us
    all_gather x1, blocking collectives, body(): right = lax.all_gather(right, 'x', tiled=True)  29.3 us
    all_to_all x1, starting transfers between devices, body(): left = lax.all_to_all(left.reshape(m * n, rows, rows), ('spot', 'z'), 0, 0)  20.5 us
    ppermute x1, waiting for transfers between devices, body(): other = lax.ppermute(mine, 'quad', swap)  15.7 us
    all_to_all x1, waiting for transfers between devices, body(): partials = lax.all_to_all(partial, 'spot', 0, 0)  13.3 us
    all_to_all x1, starting transfers between devices, body(): partials = lax.all_to_all(partial, 'spot', 0, 0)  8.77 us
    ppermute x1, starting transfers between devices, body(): other = lax.ppermute(mine, 'quad', swap)  5.49 us
    dot_general x2, matrix products, times(): lax.dot_general(l, r, (((1,), (0,)), ((), ())), preferred_element_type=F32)  3.3 us
  transfers between devices with their start and end apart: 4, of which 3 were waited for; matrix products, arithmetic and copies ran while one was open for 2% of the time, Pallas kernels for 0%

profile of v8, /device:TPU:2, one launch (start us, length us, event | category | flops | bytes accessed | tf_op | source)
XLA Modules:
  0.0 145.8 jit_solution(11974139111043362478)
XLA Ops:
  0.1 1.4 fusion.33
  1.5 0.1 copy.18
  1.6 1.1 broadcast_in_dim.30
  2.7 20.5 %all-to-all-start = ((bf16[32,112,112]{2,1,0:T(8,128)(2,1)}), bf16[32,112,112]{2,1,0:T(8,128)(2,1)S(1)}, u32[]{:S(2)}, u32[]{:S(2)}) async-start(bf16[32,112,112]{2,1,0:T(8,128)(2,1)} %bitcast.2), calls=%async_computation | async-start | bytes 1835008 | tf_op jit(solution)/shard_map/all_to_all | solution.py:43
  23.1 5.5 %collective-permute-start = (f16[112,448]{1,0:T(8,128)(2,1)S(1)}, f16[112,448]{1,0:T(8,128)(2,1)S(1)}, u32[]{:S(2)}, u32[]{:S(2)}) collective-permute-start(f16[112,448]{1,0:T(8,128)(2,1)S(1)} %get-tuple-element.13), channel_id=1, source_target_pairs={{0,64},{64,0},{1,65},{65,1},{2,66},{66,2},{3,67},{67,3},{4,68},{68... | collective-permute-start | bytes 301064 | tf_op jit(solution)/shard_map/ppermute | solution.py:41
  28.6 15.7 %collective-permute-done = f16[112,448]{1,0:T(8,128)(2,1)S(1)} collective-permute-done((f16[112,448]{1,0:T(8,128)(2,1)S(1)}, f16[112,448]{1,0:T(8,128)(2,1)S(1)}, u32[]{:S(2)}, u32[]{:S(2)}) %collective-permute-start) | collective-permute-done | bytes 100384 | tf_op jit(solution)/shard_map/ppermute | solution.py:41
  44.3 0.1 maximum_select_fusion
  44.4 29.3 %all-gather.1 = f16[1792,448]{1,0:T(8,128)(2,1)S(1)} all-gather(f16[224,448]{1,0:T(8,128)(2,1)S(1)} %maximum_select_fusion), channel_id=1, replica_groups=mesh['x'=8,'quad'=2,'spot'=4,'z'=8,'core'=2] {'x'}, dimensions={0}, use_global_device_ids=true | all-gather | bytes 1806336 | tf_op jit(solution)/shard_map/all_gather | solution.py:46
  73.7 0.0 all-to-all-done
  73.7 0.3 convert_reduce_fusion
  74.0 19.8 %all_to_all.25 = f32[16,8,128]{2,1,0:T(8,128)S(1)} all-to-all(f32[16,8,128]{2,1,0:T(8,128)S(1)} %broadcast_in_dim.31), channel_id=1, replica_groups=mesh['x'=8,'quad'=2,'spot'=4,'z'=8,'core'=2] {'x','quad'}, dimensions={0} | all-to-all | bytes 131072 | tf_op jit(solution)/shard_map/all_to_all | solution.py:25
  93.9 1.2 fusion
  95.1 1.9 %collective-permute-start.1 = (bf16[4,8,112,112]{3,2,1,0:T(8,128)(2,1)}, bf16[4,8,112,112]{3,2,1,0:T(8,128)(2,1)S(1)}, u32[]{:S(2)}, u32[]{:S(2)}) collective-permute-start(bf16[4,8,112,112]{3,2,1,0:T(8,128)(2,1)} %fusion), channel_id=1, source_target_pairs={{0,1},{1,0},{2,3},{3,2},{4,5},{5,4},{6,7},{7,6},{8,9},{9,8},{10,11... | collective-permute-start | bytes 2408456 | tf_op jit(solution)/shard_map/ppermute | solution.py:52
  97.0 0.3 dynamic-slice_convert_fusion
  97.4 1.9 %fusion.38 = f32[4,112,448]{2,1,0:T(8,128)S(1)} fusion(bf16[4,896,112]{2,1,0:T(8,128)(2,1)} %bitcast.4, bf16[896,448,1]{1,0,2:T(8,128)(2,1)S(1)} %bitcast.27), kind=kOutput, calls=%fused_computation.57 | convolution fusion | flops 359661568 | bytes 2408448 | tf_op jit(solution)/shard_map/dot_general | solution.py:58
  99.2 0.4 collective-permute-done.1
  99.7 0.0 copy-start
  99.7 1.5 fusion.2
  101.1 8.8 %all-to-all-start.2 = ((f16[4,112,448]{2,1,0:T(8,128)(2,1)}), f16[4,112,448]{2,1,0:T(8,128)(2,1)S(1)}, u32[]{:S(2)}, u32[]{:S(2)}) async-start(f16[4,112,448]{2,1,0:T(8,128)(2,1)} %fusion.2), calls=%async_computation.2 | async-start | bytes 917504 | tf_op jit(solution)/shard_map/all_to_all | solution.py:62
  109.9 13.3 %all-to-all-done.2 = f16[4,112,448]{2,1,0:T(8,128)(2,1)S(1)} async-done(((f16[4,112,448]{2,1,0:T(8,128)(2,1)}), f16[4,112,448]{2,1,0:T(8,128)(2,1)S(1)}, u32[]{:S(2)}, u32[]{:S(2)}) %all-to-all-start.2) | async-done | bytes 401440 | tf_op jit(solution)/shard_map/all_to_all | solution.py:62
  123.3 0.1 convert_reduce_fusion.1
  123.3 0.0 copy-done
  123.4 0.5 multiply_reduce_fusion
  123.9 0.1 maximum_bitcast_fusion
  123.9 10.6 %all_to_all.26 = f32[8,8,128]{2,1,0:T(8,128)S(1)} all-to-all(f32[8,8,128]{2,1,0:T(8,128)S(1)} %broadcast_in_dim.34), channel_id=1, replica_groups=mesh['x'=8,'quad'=2,'spot'=4,'z'=8,'core'=2] {'quad','spot'}, dimensions={0} | all-to-all | bytes 65536 | tf_op jit(solution)/shard_map/all_to_all | solution.py:25
  134.5 10.5 %all_to_all.27 = f32[8,8,128]{2,1,0:T(8,128)S(1)} all-to-all(f32[8,8,128]{2,1,0:T(8,128)S(1)} %broadcast_in_dim.35), channel_id=1, replica_groups=mesh['x'=8,'quad'=2,'spot'=4,'z'=8,'core'=2] {'x'}, dimensions={0} | all-to-all | bytes 65536 | tf_op jit(solution)/shard_map/all_to_all | solution.py:25
  145.0 0.1 fusion.32
  145.1 0.7 divide_convert_fusion
  (13 shorter events, 0.1 us)
Async XLA Ops:
  2.7 71.1 %all-to-all-start = ((bf16[32,112,112]{2,1,0:T(8,128)(2,1)}), bf16[32,112,112]{2,1,0:T(8,128)(2,1)S(1)}, u32[]{:S(2)}, u32[]{:S(2)}) async-start(bf16[32,112,112]{2,1,0:T(8,128)(2,1)} %bitcast.2), calls=%async_computation | async-start | bytes 1835008 | tf_op jit(solution)/shard_map/all_to_all | solution.py:43
  23.1 21.2 %collective-permute-start = (f16[112,448]{1,0:T(8,128)(2,1)S(1)}, f16[112,448]{1,0:T(8,128)(2,1)S(1)}, u32[]{:S(2)}, u32[]{:S(2)}) collective-permute-start(f16[112,448]{1,0:T(8,128)(2,1)S(1)} %get-tuple-element.13), channel_id=1, source_target_pairs={{0,64},{64,0},{1,65},{65,1},{2,66},{66,2},{3,67},{67,3},{4,68},{68... | collective-permute-start | bytes 301064 | tf_op jit(solution)/shard_map/ppermute | solution.py:41
  95.1 4.6 %collective-permute-start.1 = (bf16[4,8,112,112]{3,2,1,0:T(8,128)(2,1)}, bf16[4,8,112,112]{3,2,1,0:T(8,128)(2,1)S(1)}, u32[]{:S(2)}, u32[]{:S(2)}) collective-permute-start(bf16[4,8,112,112]{3,2,1,0:T(8,128)(2,1)} %fusion), channel_id=1, source_target_pairs={{0,1},{1,0},{2,3},{3,2},{4,5},{5,4},{6,7},{7,6},{8,9},{9,8},{10,11... | collective-permute-start | bytes 2408456 | tf_op jit(solution)/shard_map/ppermute | solution.py:52
  99.7 23.7 %copy-start = (s32[56,56]{1,0:T(8,128)S(1)}, s32[56,56]{1,0:T(8,128)}, u32[]{:S(2)}) copy-start(s32[56,56]{1,0:T(8,128)} %param.5) | copy-start | bytes 37636
  101.1 22.2 %all-to-all-start.2 = ((f16[4,112,448]{2,1,0:T(8,128)(2,1)}), f16[4,112,448]{2,1,0:T(8,128)(2,1)S(1)}, u32[]{:S(2)}, u32[]{:S(2)}) async-start(f16[4,112,448]{2,1,0:T(8,128)(2,1)} %fusion.2), calls=%async_computation.2 | async-start | bytes 917504 | tf_op jit(solution)/shard_map/all_to_all | solution.py:62
